TPU v7x, 32 devices: a whole 2x2x4 slice. The times are simulated.
32 devices in a mesh: expert: 8 (over z, y), wshard: 4 (over x, core).
Axes of the slice: x: 2, y: 2, z: 4, core: 2. Of those that a mesh axis runs over, the one named last changes fastest.
Arguments:
- tokens: bfloat16 [4096, 768], P(('expert', 'wshard')), may hold values from -6 to 6
- gain_attention: bfloat16 [768], P('wshard'), may hold values from 0.5 to 1.5
- gain_experts: bfloat16 [768], P('wshard'), may hold values from 0.5 to 1.5
- proj_inputs: bfloat16 [768, 2304], P('wshard'), may hold values from -0.21875 to 0.21875
- proj_output: bfloat16 [768, 768], P('wshard'), may hold values from -0.75 to 0.75
- bias_table: bfloat16 [32, 12], P('wshard'), may hold values from -4 to 4
- router_weight: bfloat16 [768, 16], P('wshard'), may hold values from -1 to 1
- routes: int32 [4096, 2], P(('expert', 'wshard')), may hold values from 0 to 15, as said below
- slot_index: int32 [4096, 2], P(('expert', 'wshard')), may hold values from 0 to 3, as said below
- drop_flags: int32 [4096, 2], P(('expert', 'wshard')), may hold values from 0 to 1, as said below
- expert_in: bfloat16 [16, 768, 3072], P('expert', None, 'wshard'), may hold values from -0.21875 to 0.21875
- expert_out: bfloat16 [16, 3072, 768], P('expert', 'wshard'), may hold values from -0.109375 to 0.109375
- cotangent: bfloat16 [4096, 768], P(('expert', 'wshard')), may hold values from -6 to 6
Outputs:
- output: bfloat16 [4096, 768], P(('expert', 'wshard'))
- grad_tokens: float32 [4096, 768], P(('expert', 'wshard'))
- grad_gain_attention: float32 [768], P('wshard')
- grad_gain_experts: float32 [768], P('wshard')
- grad_proj_inputs: float32 [768, 2304], P('wshard')
- grad_proj_output: float32 [768, 768], P('wshard')
- grad_bias_table: float32 [32, 12], P('wshard')
- grad_router: float32 [768, 16], P('wshard')
- grad_expert_in: float32 [16, 768, 3072], P('expert', None, 'wshard')
- grad_expert_out: float32 [16, 3072, 768], P('expert', 'wshard')
Inputs may be any that keep to these rules, and one draw needn't show every extreme that they name: `routes`: each row names two different experts; one expert, drawn from the seed and the same for all devices, is the first choice of at least 8 of the rows of every device. `slot_index`: within the rows of one device and one expert, the kept entries take slots 0, 1, 2, ... once each in order of rows, all first choices before all second choices; an entry with drop flag 1 has slot 0; some expert has all 4 slots kept on every device. `drop_flags`: 1 exactly where an entry's rank among the entries of its device and expert, counted as for the slots, is 4 or more; every device drops some entries.
All inputs are finite; a program needn't handle non-finite values.
Results may differ from a plain program's by a relative error of at most 0.012.
The roundings to bfloat16 on the way count: a program that leaves them out, or rounds other values in their place, can miss the bound.
Values may be sent and summed in bfloat16 or wider, within the bound.
No kernel may reach another device: no remote copies, remote signals or barrier semaphores. Data moves between devices by JAX's collectives and lax.ppermute only.
A program may use at most 128 MiB of HBM per device.

v0:
```python
import math

import jax
import jax.numpy as jnp
from jax import lax
from jax.experimental import pallas as pl
from jax.experimental.pallas import tpu as pltpu
from jax.sharding import PartitionSpec as P


NB = 32
MAXDIST = 128
CAP = 4
EPSILON = 1e-06
NEGATIVE = -1e30
BLOCK = 128
F32 = jnp.float32
BF16 = jnp.bfloat16


def bucket_starts():
    exact = NB // 2
    starts = list(range(exact + 1))
    for level in range(1, exact):
        starts.append(math.ceil(exact * (MAXDIST / exact) ** (level / exact) - 1e-09))
    return starts


STARTS = bucket_starts()


def exchange(value, axis, mask):
    size = lax.axis_size(axis)
    return lax.ppermute(value, axis, [(i, i ^ mask) for i in range(size)])


def gather_xor(value, axis):
    pieces = {0: value}
    bit = lax.axis_size(axis) // 2
    while bit >= 1:
        for key in list(pieces):
            pieces[key | bit] = exchange(pieces[key], axis, bit)
        bit //= 2
    return [pieces[k] for k in range(len(pieces))]


def whole(kernel, outs, *args, scratch=(), smem=1):
    return call_whole(kernel, outs, *args, scratch=scratch, smem=smem)


def call_whole(kernel, outs, *args, scratch, smem):
    specs = [pl.BlockSpec(memory_space=pltpu.SMEM)] * smem
    specs += [pl.BlockSpec(memory_space=pltpu.VMEM)] * (len(args) - smem)
    return pl.pallas_call(
        kernel,
        out_shape=[jax.ShapeDtypeStruct(s, d) for s, d in outs],
        in_specs=specs,
        out_specs=[pl.BlockSpec(memory_space=pltpu.VMEM)] * len(outs),
        scratch_shapes=list(scratch),
    )(*args)


def dot_nn(a, b):
    return lax.dot_general(a, b, (((1,), (0,)), ((), ())), preferred_element_type=F32)


def dot_nt(a, b):
    return lax.dot_general(a, b, (((1,), (1,)), ((), ())), preferred_element_type=F32)


def dot_tn(a, b):
    return lax.dot_general(a, b, (((0,), (0,)), ((), ())), preferred_element_type=F32)


def norm_scale(values):
    return lax.rsqrt(jnp.mean(values * values, axis=-1, keepdims=True) + EPSILON)


def sum_refs(refs):
    total = refs[0][...].astype(F32)
    for ref in refs[1:]:
        total = total + ref[...].astype(F32)
    return total


def distance_tile():
    rows = lax.broadcasted_iota(jnp.int32, (BLOCK, 2 * BLOCK), 0)
    cols = lax.broadcasted_iota(jnp.int32, (BLOCK, 2 * BLOCK), 1)
    return rows + BLOCK - cols


def rows_at(index, size):
    return pl.ds(pl.multiple_of(index * size, size & -size), size)


def prepare_kernel(groups, me_ref, w_ref, *outs_and_scratch):
    outs = outs_and_scratch[:groups]
    chunks = outs_and_scratch[groups]
    me = me_ref[0]
    third = w_ref.shape[1] // 3
    part = third // groups
    for d in range(groups):
        for s in range(3):
            chunks[d, :, s * part : (s + 1) * part] = w_ref[
                :, s * third + d * part : s * third + (d + 1) * part
            ]
    for k in range(groups):
        outs[k][...] = chunks[me ^ k]


def score_blocks(q, k, tile, far, qb, factor):
    blocks = []
    for kb in range(qb + 1):
        s = dot_nt(q, k[kb * BLOCK : (kb + 1) * BLOCK]) * factor
        if kb == qb:
            s = s + tile[:, BLOCK:]
        elif kb == qb - 1:
            s = s + tile[:, :BLOCK]
        else:
            s = s + far
        blocks.append(s)
    return blocks


def front_kernel(groups, heads, hs, me_ref, *refs):
    tok = refs[:groups]
    wp = refs[groups : 2 * groups]
    ext = refs[2 * groups : 3 * groups]
    outs = refs[3 * groups :]
    normed_ref, wfull_ref, proj_ref, mixed_ref, prob_ref = outs[:5]
    pieces = outs[5 : 5 + groups]
    tab_ref = outs[5 + groups]
    me = me_ref[0]
    count = tok[0].shape[0]
    wrows = wp[0].shape[0]
    length = count * groups
    extra = sum_refs(ext)
    gain = extra[12:13, :]
    tab_ref[...] = extra
    for k in range(groups):
        x = tok[k][...].astype(F32)
        normed_ref[rows_at(me ^ k, count), :] = (x * norm_scale(x) * gain).astype(BF16)
        wfull_ref[rows_at(me ^ k, wrows), :] = wp[k][...]
    proj_ref[...] = dot_nn(normed_ref[...], wfull_ref[...]).astype(BF16)
    distance = distance_tile()
    factor = hs ** (-0.5)
    part = heads * hs
    tiles = []
    fars = []
    for h in range(heads):
        row = tab_ref[pl.ds(me * heads + h, 1), :]
        tile = jnp.broadcast_to(row[:, 0:1], distance.shape)
        for n in range(1, NB):
            tile = jnp.where(distance >= STARTS[n], row[:, n : n + 1], tile)
        tiles.append(jnp.where(distance >= 0, tile, NEGATIVE))
        fars.append(row[:, NB - 1 : NB])
    for qb in range(length // BLOCK):
        span = slice(qb * BLOCK, (qb + 1) * BLOCK)
        keys = (qb + 1) * BLOCK
        mixed = []
        for h in range(heads):
            q = proj_ref[span, h * hs : (h + 1) * hs]
            k = proj_ref[:keys, part + h * hs : part + (h + 1) * hs]
            v = proj_ref[:keys, 2 * part + h * hs : 2 * part + (h + 1) * hs]
            blocks = score_blocks(q, k, tiles[h], fars[h], qb, factor)
            top = blocks[0]
            for s in blocks[1:]:
                top = jnp.maximum(top, s)
            top = jnp.max(top, axis=-1, keepdims=True)
            es = [jnp.exp(s - top) for s in blocks]
            total = es[0]
            for e in es[1:]:
                total = total + e
            total = jnp.sum(total, axis=-1, keepdims=True)
            inverse = 1.0 / total
            w = jnp.concatenate([e * inverse for e in es], axis=1)
            prob_ref[h, span, :keys] = w
            mixed.append(dot_nn(w.astype(BF16), v))
        mixed_ref[span, :] = jnp.concatenate(mixed, axis=1).astype(BF16)
    for k in range(groups):
        pieces[k][...] = mixed_ref[rows_at(me ^ k, count), :]


def columns(table_ref):
    table = jnp.transpose(table_ref[...])
    return [table[:, i : i + 1] for i in range(6)]


def places_of(cols, slots):
    ids = lax.broadcasted_iota(jnp.int32, (cols[0].shape[0], slots), 1).astype(F32)
    flat = [cols[r] * float(CAP) + cols[2 + r] for r in range(2)]
    flat = [jnp.where(cols[4 + r] == 0.0, flat[r], -1.0) for r in range(2)]
    return [(f == ids).astype(F32).astype(BF16) for f in flat]


def route_onehot(cols, experts):
    ids = lax.broadcasted_iota(jnp.int32, (cols[0].shape[0], experts), 1).astype(F32)
    return [(cols[r] == ids).astype(F32) for r in range(2)]


def middle_kernel(groups, experts, *refs):
    mixed = refs[:groups]
    wo = refs[groups : 2 * groups]
    ext = refs[2 * groups : 3 * groups]
    tok_ref, cot_ref, table_ref = refs[3 * groups : 3 * groups + 3]
    residual_ref, normed_ref, send_ref, gates_ref = refs[3 * groups + 3 :]
    cols = columns(table_ref)
    count, width = tok_ref.shape
    total = dot_nn(mixed[0][...], wo[0][...])
    for k in range(1, groups):
        total = total + dot_nn(mixed[k][...], wo[k][...])
    residual = tok_ref[...].astype(F32) + total
    residual_ref[...] = residual
    extra = sum_refs(ext)
    gain = extra[13:14, :]
    router = extra[16 : 16 + experts, :].astype(BF16)
    normed = (residual * norm_scale(residual) * gain).astype(BF16)
    normed_ref[...] = normed
    logits = dot_nt(normed, router)
    onehot = route_onehot(cols, experts)
    chosen = [jnp.sum(logits * o, axis=1, keepdims=True) for o in onehot]
    top = jnp.maximum(chosen[0], chosen[1])
    ex = [jnp.exp(c - top) for c in chosen]
    both = ex[0] + ex[1]
    gates = [e / both for e in ex]
    keep = [1.0 - cols[4], 1.0 - cols[5]]
    places = places_of(cols, experts * CAP)
    up = cot_ref[...].astype(F32)
    send_ref[:, :width] = dot_tn(places[0] + places[1], normed).astype(BF16)
    grads = dot_tn(places[0], (gates[0] * keep[0] * up).astype(BF16))
    grads = grads + dot_tn(places[1], (gates[1] * keep[1] * up).astype(BF16))
    send_ref[:, width:] = grads.astype(BF16)
    lanes = lax.broadcasted_iota(jnp.int32, (count, 128), 1)
    gates_ref[...] = jnp.where(lanes == 0, gates[0], gates[1])


def owner_mask(rows, local, j):
    index = lax.broadcasted_iota(jnp.int32, (rows, 1), 0)
    return (index // CAP) % local == j


def experts_kernel(groups, local, *refs):
    xs = refs[:groups]
    win_ref, wout_ref = refs[groups : groups + 2]
    hidden_ref, gpre_ref, send_ref, keep_ref, mid_ref, x_ref, acc_ref = refs[groups + 2 :]
    step = pl.program_id(0)
    rows = xs[0].shape[0]
    width = xs[0].shape[1] // 2

    @pl.when(step == 0)
    def _():
        for k in range(groups):
            x_ref[k * rows : (k + 1) * rows, :] = xs[k][...]
        acc_ref[...] = jnp.zeros_like(acc_ref)

    r = x_ref[:, :width]
    g = x_ref[:, width:]
    masks = [owner_mask(rows * groups, local, j) for j in range(local)]
    pre = dot_nn(r, win_ref[0])
    gh = dot_nt(g, wout_ref[0])
    for j in range(1, local):
        pre = jnp.where(masks[j], dot_nn(r, win_ref[j]), pre)
        gh = jnp.where(masks[j], dot_nt(g, wout_ref[j]), gh)
    root = math.sqrt(2.0 / math.pi)
    square = pre * pre
    th = jnp.tanh(root * (pre + 0.044715 * (square * pre)))
    cdf = 0.5 * (1.0 + th)
    hid = pre * cdf
    slope = cdf + 0.5 * pre * (1.0 - th * th) * (root * (1.0 + 3.0 * 0.044715 * square))
    gp = gh * slope
    hidden_ref[...] = hid.astype(BF16)
    gpre_ref[...] = gp.astype(BF16)
    for j in range(local):
        acc_ref[:, :width] += dot_nn(jnp.where(masks[j], hid, 0.0).astype(BF16), wout_ref[j])
        acc_ref[:, width:] += dot_nt(jnp.where(masks[j], gp, 0.0).astype(BF16), win_ref[j])

    @pl.when(step == pl.num_programs(0) - 1)
    def _():
        keep_ref[...] = acc_ref[0:rows, :]
        mid_ref[...] = acc_ref[2 * rows : 3 * rows, :]
        send_ref[0:rows, :] = acc_ref[rows : 2 * rows, :].astype(BF16)
        send_ref[rows : 2 * rows, :] = acc_ref[3 * rows : 4 * rows, :].astype(BF16)


def weights_kernel(groups, local, *refs):
    xs = refs[:groups]
    hidden_ref, gpre_ref, gin_ref, gout_ref, x_ref = refs[groups:]
    j = pl.program_id(0)
    rows = xs[0].shape[0]
    width = xs[0].shape[1] // 2

    @pl.when(pl.program_id(1) == 0)
    def _():
        for k in range(groups):
            x_ref[k * rows : (k + 1) * rows, :] = xs[k][...]

    mask = owner_mask(rows * groups, local, j)
    gp = jnp.where(mask, gpre_ref[...].astype(F32), 0.0).astype(BF16)
    hid = jnp.where(mask, hidden_ref[...].astype(F32), 0.0).astype(BF16)
    gin_ref[0] = dot_tn(x_ref[:, :width], gp)
    gout_ref[0] = dot_tn(hid, x_ref[:, width:])


def return_kernel(groups, experts, *refs):
    ext = refs[:groups]
    back_ref, residual_ref, normed_ref, gates_ref, cot_ref = refs[groups : groups + 5]
    table_ref = refs[groups + 5]
    out_ref, gres_ref, gresb_ref, small_ref = refs[groups + 6 :]
    cols = columns(table_ref)
    _, width = cot_ref.shape
    places = places_of(cols, experts * CAP)
    onehot = route_onehot(cols, experts)
    keep = [1.0 - cols[4], 1.0 - cols[5]]
    gates = [gates_ref[:, 0:1], gates_ref[:, 1:2]]
    up = cot_ref[...].astype(F32)
    residual = residual_ref[...]
    values = back_ref[:, :width]
    picked = [dot_nn(p, values) for p in places]
    moe = gates[0] * keep[0] * picked[0] + gates[1] * keep[1] * picked[1]
    out_ref[...] = (residual + moe).astype(BF16)
    gg = [keep[r] * jnp.sum(up * picked[r], axis=1, keepdims=True) for r in range(2)]
    mean = gates[0] * gg[0] + gates[1] * gg[1]
    gc = [gates[r] * (gg[r] - mean) for r in range(2)]
    glog = (onehot[0] * gc[0] + onehot[1] * gc[1]).astype(BF16)
    extra = sum_refs(ext)
    gain = extra[13:14, :]
    router = extra[16 : 16 + experts, :].astype(BF16)
    gn = dot_nn(places[0] + places[1], back_ref[:, width:]) + dot_nn(glog, router)
    scale = norm_scale(residual)
    small_ref[0:16, :] = jnp.zeros((16, width), F32)
    small_ref[13:14, :] = jnp.sum(gn * residual * scale, axis=0, keepdims=True)
    small_ref[16 : 16 + experts, :] = dot_tn(glog, normed_ref[...])
    scaled = gn * gain
    inner = jnp.mean(scaled * residual, axis=-1, keepdims=True)
    gres = up + scale * scaled - residual * (scale * scale * scale * inner)
    gres_ref[...] = gres
    gresb_ref[...] = gres.astype(BF16)


def slot_rows(ref, block, rows, me, pos, t, s):
    return ref[pl.ds(pl.multiple_of((me ^ t) * block + (pos ^ s) * rows, 8), rows), :]


def values_kernel(groups, heads, hs, slots, me_ref, *refs):
    gr = refs[:groups]
    wo_ref, mixed_ref, prob_ref, normed_ref = refs[groups : groups + 4]
    gm_ref, gv_ref, send_ref, keep_ref, grf_ref, go_ref, gi_ref = refs[groups + 4 :]
    me = me_ref[0]
    pos = me_ref[1]
    count = gr[0].shape[0]
    length = count * groups
    for k in range(groups):
        grf_ref[rows_at(me ^ k, count), :] = gr[k][...]
    gm_ref[...] = dot_nt(grf_ref[...], wo_ref[...]).astype(BF16)
    go_ref[...] = dot_tn(mixed_ref[...], grf_ref[...])
    for b in range(length // BLOCK):
        cut = slice(b * BLOCK, (b + 1) * BLOCK)
        dv = [
            dot_tn(
                prob_ref[h, b * BLOCK :, cut].astype(BF16),
                gm_ref[b * BLOCK :, h * hs : (h + 1) * hs],
            )
            for h in range(heads)
        ]
        gv_ref[cut, :] = jnp.concatenate(dv, axis=1).astype(BF16)
    gi_ref[...] = dot_tn(normed_ref[...], gv_ref[...])
    if slots == 0:
        send_ref[...] = go_ref[...].astype(BF16)
        keep_ref[...] = gi_ref[...].astype(BF16)
        return
    block = go_ref.shape[0]
    rows = block // slots
    for s in range(slots):
        own = go_ref[pl.ds(pl.multiple_of((pos ^ s) * rows, 8), rows), :]
        parts = [slot_rows(gi_ref, block, rows, me, pos, t, s) for t in range(groups)]
        both = jnp.concatenate([own, jnp.concatenate(parts, axis=1)], axis=0).astype(BF16)
        if s % 2:
            send_ref[s // 2] = both
        else:
            keep_ref[s // 2] = both


def scores_kernel(groups, heads, hs, slots, me_ref, *refs):
    tok = refs[:groups]
    gm_ref, gv_ref, proj_ref, prob_ref, normed_ref, wfull_ref = refs[groups : groups + 6]
    early_ref = refs[groups + 6]
    outs = refs[groups + 7 :]
    send_ref, keep_ref, rows_ref, own_ref, mid_ref, small_ref = outs[:6]
    gproj_ref, gi_ref, gn_ref = outs[6:]
    me = me_ref[0]
    pos = me_ref[1]
    count, width = tok[0].shape
    length = count * groups
    factor = hs ** (-0.5)
    part = heads * hs
    blocks_n = length // BLOCK
    distance = distance_tile()
    dqs = [[None] * heads for _ in range(blocks_n)]
    dks = [[None] * heads for _ in range(blocks_n)]
    tiles = []
    for h in range(heads):
        near = jnp.zeros((BLOCK, BLOCK), F32)
        prev = jnp.zeros((BLOCK, BLOCK), F32)
        rest = jnp.zeros((BLOCK, BLOCK), F32)
        for qb in range(blocks_n):
            span = slice(qb * BLOCK, (qb + 1) * BLOCK)
            keys = (qb + 1) * BLOCK
            q = proj_ref[span, h * hs : (h + 1) * hs]
            k = proj_ref[:keys, part + h * hs : part + (h + 1) * hs]
            v = proj_ref[:keys, 2 * part + h * hs : 2 * part + (h + 1) * hs]
            gm = gm_ref[span, h * hs : (h + 1) * hs]
            p = prob_ref[h, span, :keys]
            gw = dot_nt(gm, v)
            inner = jnp.sum(p * gw, axis=-1, keepdims=True)
            ds = p * (gw - inner)
            near = near + ds[:, qb * BLOCK :]
            if qb >= 1:
                prev = prev + ds[:, (qb - 1) * BLOCK : qb * BLOCK]
            for kb in range(qb - 1):
                rest = rest + ds[:, kb * BLOCK : (kb + 1) * BLOCK]
            dsb = ds.astype(BF16)
            dqs[qb][h] = dot_nn(dsb, k) * factor
            dk = dot_tn(dsb, q)
            for kb in range(qb + 1):
                cut = slice(kb * BLOCK, (kb + 1) * BLOCK)
                if dks[kb][h] is None:
                    dks[kb][h] = dk[cut]
                else:
                    dks[kb][h] = dks[kb][h] + dk[cut]
        tiles.append((jnp.concatenate([prev, near], axis=1), rest))
    for b in range(blocks_n):
        span = slice(b * BLOCK, (b + 1) * BLOCK)
        full = jnp.concatenate(dqs[b] + [d * factor for d in dks[b]], axis=1)
        gproj_ref[span, : 2 * part] = full.astype(BF16)
    gproj_ref[:, 2 * part :] = gv_ref[...]
    gi_ref[...] = dot_tn(normed_ref[...], gproj_ref[:, : 2 * part])
    if slots == 0:
        send_ref[...] = gi_ref[...].astype(BF16)
        keep_ref[...] = jnp.zeros_like(keep_ref)
    else:
        block = width // groups
        rows = block // slots
        for s in range(slots):
            parts = [slot_rows(gi_ref, block, rows, me, pos, t, s) for t in range(groups)]
            both = jnp.concatenate(parts, axis=0).astype(BF16)
            if s % 2:
                send_ref[s // 2] = both
            else:
                keep_ref[s // 2] = both
    gn_ref[...] = dot_nt(gproj_ref[...], wfull_ref[...])
    total = jnp.zeros((1, width), F32)
    for k in range(groups):
        x = tok[k][...].astype(F32)
        gn = gn_ref[rows_at(me ^ k, count), :]
        total = total + jnp.sum(gn * (x * norm_scale(x)), axis=0, keepdims=True)
        if k == 0:
            own_ref[...] = gn
        elif k == 2:
            mid_ref[...] = gn
        elif k == 1:
            rows_ref[0:count, :] = gn.astype(BF16)
        else:
            rows_ref[count : 2 * count, :] = gn.astype(BF16)
    small_ref[...] = early_ref[...]
    small_ref[12:13, :] = total
    for h in range(heads):
        tile, rest = tiles[h]
        far = jnp.sum(rest, axis=0, keepdims=True)
        far = jnp.concatenate([far, jnp.zeros_like(far)], axis=1)
        sums = []
        for n in range(NB):
            inside = distance >= STARTS[n]
            if n + 1 < NB:
                inside = inside & (distance < STARTS[n + 1])
            one = jnp.sum(jnp.where(inside, tile, 0.0), axis=0, keepdims=True)
            sums.append(one + far if n == NB - 1 else one)
        sums = jnp.transpose(jnp.concatenate(sums, axis=0))
        line = jnp.sum(sums, axis=0, keepdims=True)
        index = lax.broadcasted_iota(jnp.int32, (16, NB), 0)
        small_ref[0:16, 0:NB] += jnp.where(index == me * heads + h, line, 0.0)


def natural(pieces, me):
    out = []
    for w in range(len(pieces)):
        value = pieces[0]
        for t in range(1, len(pieces)):
            value = jnp.where((me ^ w) == t, pieces[t], value)
        out.append(value)
    return jnp.concatenate(out, axis=1)


def join_kernel(groups, me_ref, *refs):
    pieces = [r[...].astype(F32) for r in refs[:groups]]
    rest = refs[groups:-1]
    me = me_ref[0]
    if rest:
        both = [rest[0][...].astype(F32), natural(pieces, me)]
    else:
        half = pieces[0].shape[1] // 2
        both = [natural([p[:, i * half : (i + 1) * half] for p in pieces], me) for i in range(2)]
    refs[-1][...] = jnp.concatenate(both, axis=0).astype(BF16)


def final_kernel(slots, me_ref, *refs):
    first = refs[0:2]
    second = refs[2:4]
    out_ref, own_ref = refs[4:]
    pos = me_ref[1]
    rows = out_ref.shape[0] // slots
    third = out_ref.shape[1] // 3
    for s in range(slots):
        target = pl.ds(pl.multiple_of((pos ^ s) * rows, 8), rows)
        one = first[s % 2][s // 2].astype(F32)
        two = second[s % 2][s // 2].astype(F32)
        own_ref[target, :] = one[:rows]
        out_ref[target, 2 * third :] = one[rows:]
        out_ref[target, :third] = two[:rows]
        out_ref[target, third : 2 * third] = two[rows:]


def reduce_slots(send, keep, axis):
    bit = 1
    while True:
        got = exchange(send, axis, bit)
        total = keep.astype(F32) + got.astype(F32)
        if total.shape[0] == 1:
            return total[0]
        send = total[1::2].astype(BF16)
        keep = total[0::2].astype(BF16)
        bit *= 2


def spread_slots(value, axis):
    bit = lax.axis_size(axis) // 2
    while True:
        got = exchange(value, axis, bit)
        if bit == 1:
            return value, got
        value = jnp.stack([value, got], axis=1).reshape((-1,) + value.shape[1:])
        bit //= 2


def sum_all(value, axes):
    for axis in axes:
        bit = 1
        while bit < lax.axis_size(axis):
            sent = value.astype(BF16)
            value = sent.astype(F32) + exchange(sent, axis, bit).astype(F32)
            bit *= 2
    return value


def reduce_rows(send, keep, mid, axis):
    rows = keep.shape[0]
    got = exchange(send, axis, 1).astype(F32)
    other = (mid + got[rows:]).astype(BF16)
    return keep + got[:rows] + exchange(other, axis, 2).astype(F32)


def body(
    tokens,
    gain_attention,
    gain_experts,
    proj_inputs,
    proj_output,
    bias_table,
    router_weight,
    routes,
    slot_index,
    drop_flags,
    expert_in,
    expert_out,
    cotangent,
):
    groups = lax.axis_size("wshard")
    size = lax.axis_size("expert")
    me = lax.axis_index("wshard")
    pos = lax.axis_index("expert")
    where = jnp.stack([me, pos]).astype(jnp.int32)
    count, width = tokens.shape
    length = count * groups
    heads_all = bias_table.shape[1]
    heads = heads_all // groups
    hs = width // heads_all
    part = width // groups
    local = expert_in.shape[0]
    experts = local * size
    hidden_local = expert_in.shape[2]
    buckets = bias_table.shape[0] * groups

    table = jnp.concatenate(
        [routes.T, slot_index.T, drop_flags.T, jnp.zeros((2, count), jnp.int32)], axis=0
    ).astype(F32)

    extra_rows = 16 + experts
    small = jnp.zeros((extra_rows, width), BF16)
    small = lax.dynamic_update_slice(small, bias_table.T, (0, me * bias_table.shape[0]))
    small = lax.dynamic_update_slice(
        small, jnp.stack([gain_attention, gain_experts]), (12, me * part)
    )
    small = lax.dynamic_update_slice(small, router_weight.T, (16, me * part))

    tok = gather_xor(tokens, "wshard")
    chunks = whole(
        lambda *r: prepare_kernel(groups, *r),
        [((part, 3 * part), BF16)] * groups,
        where,
        proj_inputs,
        scratch=[pltpu.VMEM((groups, part, 3 * part), BF16)],
    )
    wp = [chunks[0]] + [exchange(chunks[k], "wshard", k) for k in range(1, groups)]
    ext = gather_xor(small, "wshard")
    wo = gather_xor(proj_output, "wshard")

    front = whole(
        lambda *r: front_kernel(groups, heads, hs, *r),
        [
            ((length, width), BF16),
            ((width, 3 * part), BF16),
            ((length, 3 * part), BF16),
            ((length, part), BF16),
            ((heads, length, length), F32),
        ]
        + [((count, part), BF16)] * groups,
        where,
        *tok,
        *wp,
        *ext,
        scratch=[pltpu.VMEM((extra_rows, width), F32)],
    )
    normed_one, wfull, projected, mixed, prob = front[:5]
    mine = front[5:]
    pieces = [mine[0]] + [exchange(mine[k], "wshard", k) for k in range(1, groups)]

    slots = experts * CAP
    residual, normed_two, send, gates = whole(
        lambda *r: middle_kernel(groups, experts, *r),
        [
            ((count, width), F32),
            ((count, width), BF16),
            ((slots, 2 * width), BF16),
            ((count, 128), F32),
        ],
        *pieces,
        *wo,
        *ext,
        tokens,
        cotangent,
        table,
        smem=0,
    )
    sent = lax.all_to_all(
        send.reshape(size, local * CAP, 2 * width), "expert", 0, 0, tiled=True
    ).reshape(slots, 2 * width)
    xs = gather_xor(sent, "wshard")

    rows = slots * groups
    fblock = 256
    steps = hidden_local // fblock
    full = pl.BlockSpec((slots, 2 * width), lambda f: (0, 0))
    hidden, gpre, back_send, back_keep, back_mid = pl.pallas_call(
        lambda *r: experts_kernel(groups, local, *r),
        grid=(steps,),
        in_specs=[full] * groups
        + [
            pl.BlockSpec((local, width, fblock), lambda f: (0, 0, f)),
            pl.BlockSpec((local, fblock, width), lambda f: (0, f, 0)),
        ],
        out_specs=[
            pl.BlockSpec((rows, fblock), lambda f: (0, f)),
            pl.BlockSpec((rows, fblock), lambda f: (0, f)),
            pl.BlockSpec((2 * slots, 2 * width), lambda f: (0, 0)),
            pl.BlockSpec((slots, 2 * width), lambda f: (0, 0)),
            pl.BlockSpec((slots, 2 * width), lambda f: (0, 0)),
        ],
        out_shape=[
            jax.ShapeDtypeStruct((rows, hidden_local), BF16),
            jax.ShapeDtypeStruct((rows, hidden_local), BF16),
            jax.ShapeDtypeStruct((2 * slots, 2 * width), BF16),
            jax.ShapeDtypeStruct((slots, 2 * width), F32),
            jax.ShapeDtypeStruct((slots, 2 * width), F32),
        ],
        scratch_shapes=[
            pltpu.VMEM((rows, 2 * width), BF16),
            pltpu.VMEM((rows, 2 * width), F32),
        ],
    )(*xs, expert_in, expert_out)

    full2 = pl.BlockSpec((slots, 2 * width), lambda j, f: (0, 0))
    weights_call = pl.pallas_call(
        lambda *r: weights_kernel(groups, local, *r),
        grid=(local, steps),
        in_specs=[full2] * groups
        + [
            pl.BlockSpec((rows, fblock), lambda j, f: (0, f)),
            pl.BlockSpec((rows, fblock), lambda j, f: (0, f)),
        ],
        out_specs=[
            pl.BlockSpec((1, width, fblock), lambda j, f: (j, 0, f)),
            pl.BlockSpec((1, fblock, width), lambda j, f: (j, f, 0)),
        ],
        out_shape=[
            jax.ShapeDtypeStruct(expert_in.shape, F32),
            jax.ShapeDtypeStruct(expert_out.shape, F32),
        ],
        scratch_shapes=[pltpu.VMEM((rows, 2 * width), BF16)],
    )
    grad_expert_in, grad_expert_out = weights_call(*xs, hidden, gpre)

    returned = reduce_rows(back_send, back_keep, back_mid, "wshard").astype(BF16)
    returned = lax.all_to_all(
        returned.reshape(size, local * CAP, 2 * width), "expert", 0, 0, tiled=True
    ).reshape(slots, 2 * width)

    output, grad_residual, grad_res_b, early = whole(
        lambda *r: return_kernel(groups, experts, *r),
        [
            ((count, width), BF16),
            ((count, width), F32),
            ((count, width), BF16),
            ((experts + 16, width), F32),
        ],
        *ext,
        returned,
        residual,
        normed_two,
        gates,
        cotangent,
        table,
        smem=0,
    )
    gr = gather_xor(grad_res_b, "wshard")
    fast = part % (8 * size) == 0
    cuts = size if fast else 0
    step = part // size
    first_shapes = [((part, width), BF16), ((width, part), BF16)]
    second_shapes = [((width, 2 * part), BF16), ((8, 128), BF16)]
    if fast:
        first_shapes = [((size // 2, 2 * step, width), BF16)] * 2
        second_shapes = [((size // 2, groups * step, 2 * part), BF16)] * 2
    gm, gv, first_send, first_keep = whole(
        lambda *r: values_kernel(groups, heads, hs, cuts, *r),
        [((length, part), BF16), ((length, part), BF16)] + first_shapes,
        where,
        *gr,
        proj_output,
        mixed,
        prob,
        normed_one,
        scratch=[
            pltpu.VMEM((length, width), BF16),
            pltpu.VMEM((part, width), F32),
            pltpu.VMEM((width, part), F32),
        ],
    )
    second_send, second_keep, gn_send, gn_keep, gn_mid, sums = whole(
        lambda *r: scores_kernel(groups, heads, hs, cuts, *r),
        second_shapes
        + [
            ((2 * count, width), BF16),
            ((count, width), F32),
            ((count, width), F32),
            ((experts + 16, width), F32),
        ],
        where,
        *tok,
        gm,
        gv,
        projected,
        prob,
        normed_one,
        wfull,
        early,
        scratch=[
            pltpu.VMEM((length, 3 * part), BF16),
            pltpu.VMEM((width, 2 * part), F32),
            pltpu.VMEM((length, width), F32),
        ],
    )
    grad_normed_one = reduce_rows(gn_send, gn_keep, gn_mid, "wshard")
    inputs = tokens.astype(F32)
    scale_one = norm_scale(inputs)
    gain_one_f = sum(e[12:13].astype(F32) for e in ext)
    scaled = grad_normed_one * gain_one_f
    inner = jnp.mean(scaled * inputs, axis=-1, keepdims=True)
    grad_tokens = grad_residual + (
        scale_one * scaled - inputs * scale_one * scale_one * scale_one * inner
    )

    sums = sum_all(sums, ("wshard", "expert"))
    grad_router = lax.dynamic_slice(sums[16:], (0, me * part), (experts, part)).T
    grad_gain_two = lax.dynamic_slice(sums[13], (me * part,), (part,))
    grad_gain_one = lax.dynamic_slice(sums[12], (me * part,), (part,))
    per = buckets // groups
    grad_table = lax.dynamic_slice(sums, (0, me * per), (heads_all, per)).T

    if fast:
        one = reduce_slots(first_send, first_keep, "expert").astype(BF16)
        cut = [one[step:, t * part : (t + 1) * part] for t in range(groups)]
        cut = [cut[0]] + [exchange(cut[t], "wshard", t) for t in range(1, groups)]
        one = whole(
            lambda *r: join_kernel(groups, *r),
            [((2 * step, width), BF16)],
            where,
            *cut,
            one[:step],
        )[0]
        one = spread_slots(one[None], "expert")
        two = reduce_slots(second_send, second_keep, "expert").astype(BF16)
        cut = [two[t * step : (t + 1) * step] for t in range(groups)]
        cut = [cut[0]] + [exchange(cut[t], "wshard", t) for t in range(1, groups)]
        two = whole(
            lambda *r: join_kernel(groups, *r), [((2 * step, width), BF16)], where, *cut
        )[0]
        two = spread_slots(two[None], "expert")
        total_inputs, total_output = whole(
            lambda *r: final_kernel(size, *r),
            [((part, 3 * width), F32), ((part, width), F32)],
            where,
            *one,
            *two,
        )
    else:
        total_output = lax.psum(first_send.astype(F32), "expert")
        total = jnp.concatenate([second_send, first_keep], axis=1)
        total = lax.psum(total, "expert").reshape(groups, part, 3, part)
        total = lax.all_to_all(total, "wshard", 0, 0, tiled=True)
        total_inputs = total.transpose(1, 2, 0, 3).reshape(part, 3 * width).astype(F32)
    return (
        output,
        grad_tokens,
        grad_gain_one,
        grad_gain_two,
        total_inputs,
        total_output,
        grad_table,
        grad_router,
        grad_expert_in,
        grad_expert_out,
    )


def solution(mesh):
    placed = (
        P(("expert", "wshard"), None),
        P("wshard"),
        P("wshard"),
        P("wshard", None),
        P("wshard", None),
        P("wshard", None),
        P("wshard", None),
        P(("expert", "wshard"), None),
        P(("expert", "wshard"), None),
        P(("expert", "wshard"), None),
        P("expert", None, "wshard"),
        P("expert", "wshard", None),
        P(("expert", "wshard"), None),
    )
    return jax.shard_map(
        body,
        mesh=mesh,
        in_specs=placed,
        out_specs=(
            P(("expert", "wshard"), None),
            P(("expert", "wshard"), None),
            P("wshard"),
            P("wshard"),
            P("wshard", None),
            P("wshard", None),
            P("wshard", None),
            P("wshard", None),
            P("expert", None, "wshard"),
            P("expert", "wshard", None),
        ),
        check_vma=False,
    )
```

profile of v0, /device:TPU:0, one launch (start us, length us, event | category | flops | bytes accessed | tf_op | source)
XLA Modules:
  0.0 214.2 jit_solution(2981097966327730146)
XLA Ops:
  0.6 3.0 %collective-permute-start.4 = (bf16[128,768]{1,0:T(8,128)(2,1)}, bf16[128,768]{1,0:T(8,128)(2,1)S(1)}, u32[]{:S(2)}, u32[]{:S(2)}) collective-permute-start(bf16[128,768]{1,0:T(8,128)(2,1)} %r_1_.5), channel_id=1, source_target_pairs={{0,2},{1,3},{2,0},{3,1},{4,6},{5,7},{6,4},{7,5},{8,10},{9,11},{10,... | collective-permute-start | bytes 589832 | tf_op jit(solution)/shard_map/ppermute | solution.py:34
  6.7 1.7 dynamic_update_slice.11.r_9_.r_8_.r_0_
  9.2 1.8 collective-permute-start.13
  11.7 2.4 %shard_map.204 = (bf16[192,576]{1,0:T(8,128)(2,1)}, bf16[192,576]{1,0:T(8,128)(2,1)}, bf16[192,576]{1,0:T(8,128)(2,1)}, bf16[192,576]{1,0:T(8,128)(2,1)}) custom-call(s32[2]{0:T(128)} %pad_add_fusion.r_0_, bf16[192,2304]{1,0:T(8,128)(2,1)} %r_1_.3), custom_call_target="tpu_custom_call" | custom-call | tf_op jit(solution)/shard_map/pallas_call | solution.py:54
  14.6 1.3 collective-permute-done.2.r_12_.r_11_.r_3_
  16.1 1.3 collective-permute-start.8
  19.1 5.8 %collective-permute-done.7.r_7_ = bf16[192,576]{1,0:T(8,128)(2,1)S(1)} collective-permute-done((bf16[192,576]{1,0:T(8,128)(2,1)}, bf16[192,576]{1,0:T(8,128)(2,1)S(1)}, u32[]{:S(2)}, u32[]{:S(2)}) %collective-permute-start.7) | collective-permute-done | bytes 221216 | tf_op jit(solution)/shard_map/ppermute | solution.py:34
  24.9 3.8 %collective-permute-done.8.r_8_ = bf16[192,576]{1,0:T(8,128)(2,1)S(1)} collective-permute-done((bf16[192,576]{1,0:T(8,128)(2,1)}, bf16[192,576]{1,0:T(8,128)(2,1)S(1)}, u32[]{:S(2)}, u32[]{:S(2)}) %collective-permute-start.8) | collective-permute-done | bytes 221216 | tf_op jit(solution)/shard_map/ppermute | solution.py:34
  29.5 9.3 %shard_map.205 = (bf16[512,768]{1,0:T(8,128)(2,1)}, bf16[768,576]{1,0:T(8,128)(2,1)}, bf16[512,576]{1,0:T(8,128)(2,1)}, bf16[512,192]{1,0:T(8,128)(2,1)}, f32[3,...) custom-call(s32[2]{0:T(128)} %pad_add_fusion.r_0_, ...), custom_call_target="tpu_custom_call" | custom-call | tf_op jit(solution)/shard_map/pallas_call | solution.py:54
  39.4 1.3 collective-permute-start.10
  40.8 1.4 add_convert_fusion.10.r_14_.r_9_
  42.2 1.7 collective-permute-done.10.r_2_
  43.9 1.4 collective-permute-done.11.r_3_
  46.1 3.4 %shard_map.206 = (f32[128,768]{1,0:T(8,128)}, bf16[128,768]{1,0:T(8,128)(2,1)}, bf16[64,1536]{1,0:T(8,128)(2,1)}, f32[128,128]{1,0:T(8,128)}) custom-call(bf16[128,192]{1,0:T(8,128)(2,1)} %get-tuple-element.54.r_0_, bf16[128,192]{1,0:T(8,128)(2,1)} %copy-done.29, bf16[128,192]{1,0:T(8,128)(2,1)} %copy-done.30, bf16[128,192]{1,0:T(8,128)(2,1)} %copy-done.31, ...), custom_call_target="tpu_custom_call" | custom-call | tf_op jit(solution)/shard_map/pallas_call | solution.py:54
  49.5 14.0 %all_to_all.10 = bf16[8,8,1536]{2,1,0:T(8,128)(2,1)S(1)} all-to-all(bf16[8,8,1536]{2,1,0:T(8,128)(2,1)} %bitcast.61), channel_id=1, replica_groups=mesh['expert'=8,'wshard'=4] {'expert'}, dimensions={0} | all-to-all | bytes 393216 | tf_op jit(solution)/shard_map/all_to_all | solution.py:653
  64.6 4.6 %collective-permute-done.16.r_2_ = bf16[64,1536]{1,0:T(8,128)(2,1)S(1)} collective-permute-done((bf16[64,1536]{1,0:T(8,128)(2,1)S(1)}, bf16[64,1536]{1,0:T(8,128)(2,1)S(1)}, u32[]{:S(2)}, u32[]{:S(2)}) %collective-permute-start.16) | collective-permute-done | bytes 196640 | tf_op jit(solution)/shard_map/ppermute | solution.py:34
  69.2 1.4 collective-permute-done.17.r_3_
  71.3 6.8 %shard_map.207 = (bf16[256,768]{1,0:T(8,128)(2,1)}, bf16[256,768]{1,0:T(8,128)(2,1)}, bf16[128,1536]{1,0:T(8,128)(2,1)}, f32[64,1536]{1,0:T(8,128)}, f32[64,1536]{1,0:T(8,128)}) custom-call(bf16[64,1536]{1,0:T(8,128)(2,1)} %bitcast.49, bf16[64,1536]{1,0:T(8,128)(2,1)} %copy-done.10, bf16[64,1536]{1,0:T(8,128)(2,1)} %copy-done.9, ...), custom_call_target="tpu_custom_call" | custom-call | tf_op jit(solution)/shard_map/pallas_call | solution.py:662
  78.3 1.8 collective-permute-done.18
  82.4 5.9 %collective-permute-done.19 = bf16[64,1536]{1,0:T(8,128)(2,1)S(1)} collective-permute-done((bf16[64,1536]{1,0:T(8,128)(2,1)S(1)}, bf16[64,1536]{1,0:T(8,128)(2,1)S(1)}, u32[]{:S(2)}, u32[]{:S(2)}) %collective-permute-start.19) | collective-permute-done | bytes 196640 | tf_op jit(solution)/shard_map/ppermute | solution.py:34
  89.3 11.6 %all_to_all.11 = bf16[8,8,1536]{2,1,0:T(8,128)(2,1)} all-to-all(bf16[8,8,1536]{2,1,0:T(8,128)(2,1)S(1)} %fusion.13), channel_id=1, replica_groups=mesh['expert'=8,'wshard'=4] {'expert'}, dimensions={0} | all-to-all | bytes 393216 | tf_op jit(solution)/shard_map/all_to_all | solution.py:712
  100.9 3.6 %shard_map.208 = (bf16[128,768]{1,0:T(8,128)(2,1)}, f32[128,768]{1,0:T(8,128)}, bf16[128,768]{1,0:T(8,128)(2,1)}, f32[32,768]{1,0:T(8,128)}) custom-call(bf16[32,768]{1,0:T(8,128)(2,1)} %copy-done.5, bf16[32,768]{1,0:T(8,128)(2,1)} %copy-done.13, bf16[32,768]{1,0:T(8,128)(2,1)} %copy-done.12, bf16[32,768]{1,0:T(8,128)(2,1)} %copy-done.14, ...), custom_call_target="tpu_custom_call" | custom-call | tf_op jit(solution)/shard_map/pallas_call | solution.py:54
  105.5 4.9 %collective-permute-done.21.r_3_ = bf16[128,768]{1,0:T(8,128)(2,1)S(1)} collective-permute-done((bf16[128,768]{1,0:T(8,128)(2,1)}, bf16[128,768]{1,0:T(8,128)(2,1)S(1)}, u32[]{:S(2)}, u32[]{:S(2)}) %collective-permute-start.21) | collective-permute-done | bytes 196640 | tf_op jit(solution)/shard_map/ppermute | solution.py:34
  110.4 1.4 collective-permute-done.22.r_4_
  112.5 5.2 %shard_map.209 = (bf16[512,192]{1,0:T(8,128)(2,1)}, bf16[512,192]{1,0:T(8,128)(2,1)}, bf16[4,48,768]{2,1,0:T(8,128)(2,1)}, bf16[4,48,768]{2,1,0:T(8,128)(2,1)}) custom-call(s32[2]{0:T(128)} %pad_add_fusion.r_0_, bf16[128,768]{1,0:T(8,128)(2,1)} %get-tuple-element.67.r_1_, bf16[128,768]{1,0:T(8,128)(2,1)} %copy-done.27, bf16[128,768]{1,0:T(8,128)(2,1)} %copy-done.26, ...), custom_call_target="tpu_custom_call" | custom-call | tf_op jit(solution)/shard_map/pallas_call | solution.py:54
  117.7 8.5 %shard_map.210 = (bf16[4,96,384]{2,1,0:T(8,128)(2,1)}, bf16[4,96,384]{2,1,0:T(8,128)(2,1)}, bf16[256,768]{1,0:T(8,128)(2,1)}, f32[128,768]{1,0:T(8,128)}, f32[128,768]{1,0:T(8,128)}, /*index=5*/f32[32,768]{1,0:T(8,128)}) custom-call(s32[2]{0:T(128)} %pad_add_fusion.r_0_, bf16[128,768]{1,0:T(8,128)(2,1)} %r_1_.5, bf16[128,768]{1,0:T(8,128)(2,1)} %copy-done.7, ...), custom_call_target="tpu_custom_call" | custom-call | tf_op jit(solution)/shard_map/pallas_call | solution.py:54
  130.4 3.1 %collective-permute-done.26 = bf16[32,768]{1,0:T(8,128)(2,1)S(1)} collective-permute-done((bf16[32,768]{1,0:T(8,128)(2,1)S(1)}, bf16[32,768]{1,0:T(8,128)(2,1)S(1)}, u32[]{:S(2)}, u32[]{:S(2)}) %collective-permute-start.26) | collective-permute-done | bytes 49184 | tf_op jit(solution)/shard_map/ppermute | solution.py:34
  134.5 3.1 %collective-permute-done.27 = bf16[32,768]{1,0:T(8,128)(2,1)S(1)} collective-permute-done((bf16[32,768]{1,0:T(8,128)(2,1)S(1)}, bf16[32,768]{1,0:T(8,128)(2,1)S(1)}, u32[]{:S(2)}, u32[]{:S(2)}) %collective-permute-start.27) | collective-permute-done | bytes 49184 | tf_op jit(solution)/shard_map/ppermute | solution.py:34
  137.9 3.9 %collective-permute-done.28 = bf16[32,768]{1,0:T(8,128)(2,1)S(1)} collective-permute-done((bf16[32,768]{1,0:T(8,128)(2,1)S(1)}, bf16[32,768]{1,0:T(8,128)(2,1)S(1)}, u32[]{:S(2)}, u32[]{:S(2)}) %collective-permute-start.28) | collective-permute-done | bytes 49184 | tf_op jit(solution)/shard_map/ppermute | solution.py:34
  143.2 7.5 %shard_map.214 = (f32[2,768,768]{2,1,0:T(8,128)}, f32[2,768,768]{2,1,0:T(8,128)}) custom-call(bf16[64,1536]{1,0:T(8,128)(2,1)} %bitcast.50, bf16[64,1536]{1,0:T(8,128)(2,1)} %copy-done.10, bf16[64,1536]{1,0:T(8,128)(2,1)} %copy-done.9, bf16[64,1536]{1,0:T(8,128)(2,1)} %copy-done.11, bf16[256,768]{1,0:T(8,128)(2,1)} %get-tuple-element.86.r_4_, ...), custom_call_target="tpu_custom_call" | custom-call | tf_op jit(solution)/shard_map/pallas_call | solution.py:709
  151.2 1.6 collective-permute-start.30
  154.9 4.6 %collective-permute-done.39 = bf16[4,96,384]{2,1,0:T(8,128)(2,1)S(1)} collective-permute-done((bf16[4,96,384]{2,1,0:T(8,128)(2,1)}, bf16[4,96,384]{2,1,0:T(8,128)(2,1)S(1)}, u32[]{:S(2)}, u32[]{:S(2)}) %collective-permute-start.39) | collective-permute-done | bytes 294944 | tf_op jit(solution)/shard_map/ppermute | solution.py:34
  161.3 1.3 collective-permute-done.30
  163.5 3.0 %collective-permute-done.40 = bf16[2,96,384]{2,1,0:T(8,128)(2,1)S(1)} collective-permute-done((bf16[2,96,384]{2,1,0:T(8,128)(2,1)S(1)}, bf16[2,96,384]{2,1,0:T(8,128)(2,1)S(1)}, u32[]{:S(2)}, u32[]{:S(2)}) %collective-permute-start.40) | collective-permute-done | bytes 147488 | tf_op jit(solution)/shard_map/ppermute | solution.py:34
  166.6 2.4 %collective-permute-start.41 = (bf16[1,96,384]{2,1,0:T(8,128)(2,1)S(1)}, bf16[1,96,384]{2,1,0:T(8,128)(2,1)S(1)}, u32[]{:S(2)}, u32[]{:S(2)}) collective-permute-start(bf16[1,96,384]{2,1,0:T(8,128)(2,1)S(1)} %slice.162), channel_id=1, source_target_pairs={{0,16},{4,20},{8,24},{12,28},{16,0},{20,4},{24,8},{28,12},{1,17},{... | collective-permute-start | bytes 221192 | tf_op jit(solution)/shard_map/ppermute | solution.py:34
  169.1 1.5 collective-permute-start.32
  170.6 2.0 collective-permute-done.41
  173.2 1.9 collective-permute-done.32
  180.8 1.6 shard_map.211
  184.8 1.5 shard_map.212
  186.4 2.2 %collective-permute-start.45 = (bf16[1,48,768]{2,1,0:T(8,128)(2,1)}, bf16[1,48,768]{2,1,0:T(8,128)(2,1)S(1)}, u32[]{:S(2)}, u32[]{:S(2)}) collective-permute-start(bf16[1,48,768]{2,1,0:T(8,128)(2,1)} %bitcast.59), channel_id=1, source_target_pairs={{0,16},{4,20},{8,24},{12,28},{16,0},{20,4},{24,8},{28,12},{1,17},{... | collective-permute-start | bytes 221192 | tf_op jit(solution)/shard_map/ppermute | solution.py:34
  189.8 3.7 %collective-permute-done.45 = bf16[1,48,768]{2,1,0:T(8,128)(2,1)S(1)} collective-permute-done((bf16[1,48,768]{2,1,0:T(8,128)(2,1)}, bf16[1,48,768]{2,1,0:T(8,128)(2,1)S(1)}, u32[]{:S(2)}, u32[]{:S(2)}) %collective-permute-start.45) | collective-permute-done | bytes 73760 | tf_op jit(solution)/shard_map/ppermute | solution.py:34
  194.8 1.8 collective-permute-done.37
  196.7 1.3 collective-permute-start.38
  198.0 1.6 collective-permute-done.46
  201.7 5.0 %collective-permute-done.38.r_2_ = bf16[4,48,768]{2,1,0:T(8,128)(2,1)S(1)} collective-permute-done((bf16[4,48,768]{2,1,0:T(8,128)(2,1)S(1)}, bf16[4,48,768]{2,1,0:T(8,128)(2,1)S(1)}, u32[]{:S(2)}, u32[]{:S(2)}) %collective-permute-start.38) | collective-permute-done | bytes 294944 | tf_op jit(solution)/shard_map/ppermute | solution.py:34
  206.6 4.0 %collective-permute-done.47.r_4_ = bf16[4,48,768]{2,1,0:T(8,128)(2,1)S(1)} collective-permute-done((bf16[4,48,768]{2,1,0:T(8,128)(2,1)S(1)}, bf16[4,48,768]{2,1,0:T(8,128)(2,1)S(1)}, u32[]{:S(2)}, u32[]{:S(2)}) %collective-permute-start.47) | collective-permute-done | bytes 294944 | tf_op jit(solution)/shard_map/ppermute | solution.py:34
  211.4 2.8 %shard_map.213 = (f32[192,2304]{1,0:T(8,128)}, f32[192,768]{1,0:T(8,128)}) custom-call(s32[2]{0:T(128)} %pad_add_fusion.r_0_, bf16[4,48,768]{2,1,0:T(8,128)(2,1)} %bitcast.52, bf16[4,48,768]{2,1,0:T(8,128)(2,1)} %copy-done.21, bf16[4,48,768]{2,1,0:T(8,128)(2,1)} %bitcast.54, bf16[4,48,768]{2,1,0:T(8,128)(2,1)} %copy-done.22), custom_call_target="tpu_custom_call" | custom-call | tf_op jit(solution)/shard_map/pallas_call | solution.py:54
  (191 shorter events, 42.3 us)
Async XLA Ops:
  0.6 15.4 %collective-permute-start.4 = (bf16[128,768]{1,0:T(8,128)(2,1)}, bf16[128,768]{1,0:T(8,128)(2,1)S(1)}, u32[]{:S(2)}, u32[]{:S(2)}) collective-permute-start(bf16[128,768]{1,0:T(8,128)(2,1)} %r_1_.5), channel_id=1, source_target_pairs={{0,2},{1,3},{2,0},{3,1},{4,6},{5,7},{6,4},{7,5},{8,10},{9,11},{10,... | collective-permute-start | bytes 589832 | tf_op jit(solution)/shard_map/ppermute | solution.py:34
  8.4 5.6 %collective-permute-start.1 = (bf16[32,768]{1,0:T(8,128)(2,1)S(1)}, bf16[32,768]{1,0:T(8,128)(2,1)S(1)}, u32[]{:S(2)}, u32[]{:S(2)}) collective-permute-start(bf16[32,768]{1,0:T(8,128)(2,1)S(1)} %dynamic_update_slice.11.r_9_.r_8_.r_0_), channel_id=1, source_target_pairs={{0,2},{1,3},{2,0},{3,1},{4,6},{5,7},{6,4},{7,5},{8,10},{9,11},{10,... | collective-permute-start | bytes 147464 | tf_op jit(solution)/shard_map/ppermute | solution.py:34
  8.7 5.4 %collective-permute-start = (bf16[32,768]{1,0:T(8,128)(2,1)S(1)}, bf16[32,768]{1,0:T(8,128)(2,1)S(1)}, u32[]{:S(2)}, u32[]{:S(2)}) collective-permute-start(bf16[32,768]{1,0:T(8,128)(2,1)S(1)} %dynamic_update_slice.11.r_9_.r_8_.r_0_), channel_id=1, source_target_pairs={{0,1},{1,0},{2,3},{3,2},{4,5},{5,4},{6,7},{7,6},{8,9},{9,8},{10,11... | collective-permute-start | bytes 147464 | tf_op jit(solution)/shard_map/ppermute | solution.py:34
  8.9 8.4 %collective-permute-start.3 = (bf16[128,768]{1,0:T(8,128)(2,1)}, bf16[128,768]{1,0:T(8,128)(2,1)S(1)}, u32[]{:S(2)}, u32[]{:S(2)}) collective-permute-start(bf16[128,768]{1,0:T(8,128)(2,1)} %r_1_.5), channel_id=1, source_target_pairs={{0,1},{1,0},{2,3},{3,2},{4,5},{5,4},{6,7},{7,6},{8,9},{9,8},{10,11... | collective-permute-start | bytes 589832 | tf_op jit(solution)/shard_map/ppermute | solution.py:34
  9.2 9.8 %collective-permute-start.13 = (bf16[192,768]{1,0:T(8,128)(2,1)}, bf16[192,768]{1,0:T(8,128)(2,1)S(1)}, u32[]{:S(2)}, u32[]{:S(2)}) collective-permute-start(bf16[192,768]{1,0:T(8,128)(2,1)} %r_5_.3), channel_id=1, source_target_pairs={{0,2},{1,3},{2,0},{3,1},{4,6},{5,7},{6,4},{7,5},{8,10},{9,11},{10,... | collective-permute-start | bytes 884744 | tf_op jit(solution)/shard_map/ppermute | solution.py:34
  14.0 4.0 %collective-permute-start.6 = (bf16[192,576]{1,0:T(8,128)(2,1)}, bf16[192,576]{1,0:T(8,128)(2,1)S(1)}, u32[]{:S(2)}, u32[]{:S(2)}) collective-permute-start(bf16[192,576]{1,0:T(8,128)(2,1)} %get-tuple-element.51), channel_id=1, source_target_pairs={{0,1},{1,0},{2,3},{3,2},{4,5},{5,4},{6,7},{7,6},{8,9},{9,8},{10,11... | collective-permute-start | bytes 663560 | tf_op jit(solution)/shard_map/ppermute | solution.py:34
  14.1 1.8 collective-permute-start.2
  15.8 9.0 %collective-permute-start.7 = (bf16[192,576]{1,0:T(8,128)(2,1)}, bf16[192,576]{1,0:T(8,128)(2,1)S(1)}, u32[]{:S(2)}, u32[]{:S(2)}) collective-permute-start(bf16[192,576]{1,0:T(8,128)(2,1)} %get-tuple-element.52), channel_id=1, source_target_pairs={{0,2},{1,3},{2,0},{3,1},{4,6},{5,7},{6,4},{7,5},{8,10},{9,11},{10,... | collective-permute-start | bytes 663560 | tf_op jit(solution)/shard_map/ppermute | solution.py:34
  16.1 12.6 %collective-permute-start.8 = (bf16[192,576]{1,0:T(8,128)(2,1)}, bf16[192,576]{1,0:T(8,128)(2,1)S(1)}, u32[]{:S(2)}, u32[]{:S(2)}) collective-permute-start(bf16[192,576]{1,0:T(8,128)(2,1)} %get-tuple-element.53), channel_id=1, source_target_pairs={{0,3},{1,2},{2,1},{3,0},{4,7},{5,6},{6,5},{7,4},{8,11},{9,10},{10,... | collective-permute-start | bytes 663560 | tf_op jit(solution)/shard_map/ppermute | solution.py:34
  17.3 11.3 %collective-permute-start.5 = (bf16[128,768]{1,0:T(8,128)(2,1)S(1)}, bf16[128,768]{1,0:T(8,128)(2,1)S(1)}, u32[]{:S(2)}, u32[]{:S(2)}) collective-permute-start(bf16[128,768]{1,0:T(8,128)(2,1)S(1)} %collective-permute-done.4.r_3_), channel_id=1, source_target_pairs={{0,1},{1,0},{2,3},{3,2},{4,5},{5,4},{6,7},{7,6},{8,9},{9,8},{10,11... | collective-permute-start | bytes 589832 | tf_op jit(solution)/shard_map/ppermute | solution.py:34
  18.0 24.2 %collective-permute-start.12 = (bf16[192,768]{1,0:T(8,128)(2,1)}, bf16[192,768]{1,0:T(8,128)(2,1)S(1)}, u32[]{:S(2)}, u32[]{:S(2)}) collective-permute-start(bf16[192,768]{1,0:T(8,128)(2,1)} %r_5_.3), channel_id=1, source_target_pairs={{0,1},{1,0},{2,3},{3,2},{4,5},{5,4},{6,7},{7,6},{8,9},{9,8},{10,11... | collective-permute-start | bytes 884744 | tf_op jit(solution)/shard_map/ppermute | solution.py:34
  19.0 26.3 %collective-permute-start.14 = (bf16[192,768]{1,0:T(8,128)(2,1)S(1)}, bf16[192,768]{1,0:T(8,128)(2,1)S(1)}, u32[]{:S(2)}, u32[]{:S(2)}) collective-permute-start(bf16[192,768]{1,0:T(8,128)(2,1)S(1)} %collective-permute-done.13.r_6_), channel_id=1, source_target_pairs={{0,1},{1,0},{2,3},{3,2},{4,5},{5,4},{6,7},{7,6},{8,9},{9,8},{10,11... | collective-permute-start | bytes 884744 | tf_op jit(solution)/shard_map/ppermute | solution.py:34
  38.8 3.4 %collective-permute-start.9 = (bf16[128,192]{1,0:T(8,128)(2,1)}, bf16[128,192]{1,0:T(8,128)(2,1)S(1)}, u32[]{:S(2)}, u32[]{:S(2)}) collective-permute-start(bf16[128,192]{1,0:T(8,128)(2,1)} %get-tuple-element.55), channel_id=1, source_target_pairs={{0,1},{1,0},{2,3},{3,2},{4,5},{5,4},{6,7},{7,6},{8,9},{9,8},{10,11... | collective-permute-start | bytes 147464 | tf_op jit(solution)/shard_map/ppermute | solution.py:34
  39.4 4.5 %collective-permute-start.10 = (bf16[128,192]{1,0:T(8,128)(2,1)}, bf16[128,192]{1,0:T(8,128)(2,1)S(1)}, u32[]{:S(2)}, u32[]{:S(2)}) collective-permute-start(bf16[128,192]{1,0:T(8,128)(2,1)} %get-tuple-element.56), channel_id=1, source_target_pairs={{0,2},{1,3},{2,0},{3,1},{4,6},{5,7},{6,4},{7,5},{8,10},{9,11},{10,... | collective-permute-start | bytes 147464 | tf_op jit(solution)/shard_map/ppermute | solution.py:34
  40.7 4.6 %collective-permute-start.11 = (bf16[128,192]{1,0:T(8,128)(2,1)}, bf16[128,192]{1,0:T(8,128)(2,1)S(1)}, u32[]{:S(2)}, u32[]{:S(2)}) collective-permute-start(bf16[128,192]{1,0:T(8,128)(2,1)} %get-tuple-element.57), channel_id=1, source_target_pairs={{0,3},{1,2},{2,1},{3,0},{4,7},{5,6},{6,5},{7,4},{8,11},{9,10},{10,... | collective-permute-start | bytes 147464 | tf_op jit(solution)/shard_map/ppermute | solution.py:34
  63.5 5.7 %collective-permute-start.16 = (bf16[64,1536]{1,0:T(8,128)(2,1)S(1)}, bf16[64,1536]{1,0:T(8,128)(2,1)S(1)}, u32[]{:S(2)}, u32[]{:S(2)}) collective-permute-start(bf16[64,1536]{1,0:T(8,128)(2,1)S(1)} %bitcast.47), channel_id=1, source_target_pairs={{0,2},{1,3},{2,0},{3,1},{4,6},{5,7},{6,4},{7,5},{8,10},{9,11},{10,... | collective-permute-start | bytes 589832 | tf_op jit(solution)/shard_map/ppermute | solution.py:34
  64.6 4.6 %collective-permute-start.15 = (bf16[64,1536]{1,0:T(8,128)(2,1)S(1)}, bf16[64,1536]{1,0:T(8,128)(2,1)S(1)}, u32[]{:S(2)}, u32[]{:S(2)}) collective-permute-start(bf16[64,1536]{1,0:T(8,128)(2,1)S(1)} %bitcast.48), channel_id=1, source_target_pairs={{0,1},{1,0},{2,3},{3,2},{4,5},{5,4},{6,7},{7,6},{8,9},{9,8},{10,11... | collective-permute-start | bytes 589832 | tf_op jit(solution)/shard_map/ppermute | solution.py:34
  69.2 1.4 collective-permute-start.17
  78.1 2.0 collective-permute-start.18
  81.3 7.0 %collective-permute-start.19 = (bf16[64,1536]{1,0:T(8,128)(2,1)S(1)}, bf16[64,1536]{1,0:T(8,128)(2,1)S(1)}, u32[]{:S(2)}, u32[]{:S(2)}) collective-permute-start(bf16[64,1536]{1,0:T(8,128)(2,1)S(1)} %fusion.10), channel_id=1, source_target_pairs={{0,2},{1,3},{2,0},{3,1},{4,6},{5,7},{6,4},{7,5},{8,10},{9,11},{10,... | collective-permute-start | bytes 589832 | tf_op jit(solution)/shard_map/ppermute | solution.py:34
  104.5 5.9 %collective-permute-start.21 = (bf16[128,768]{1,0:T(8,128)(2,1)}, bf16[128,768]{1,0:T(8,128)(2,1)S(1)}, u32[]{:S(2)}, u32[]{:S(2)}) collective-permute-start(bf16[128,768]{1,0:T(8,128)(2,1)} %get-tuple-element.67.r_1_), channel_id=1, source_target_pairs={{0,2},{1,3},{2,0},{3,1},{4,6},{5,7},{6,4},{7,5},{8,10},{9,11},{10,... | collective-permute-start | bytes 589832 | tf_op jit(solution)/shard_map/ppermute | solution.py:34
  105.5 4.9 %collective-permute-start.20 = (bf16[128,768]{1,0:T(8,128)(2,1)}, bf16[128,768]{1,0:T(8,128)(2,1)S(1)}, u32[]{:S(2)}, u32[]{:S(2)}) collective-permute-start(bf16[128,768]{1,0:T(8,128)(2,1)} %get-tuple-element.67.r_1_), channel_id=1, source_target_pairs={{0,1},{1,0},{2,3},{3,2},{4,5},{5,4},{6,7},{7,6},{8,9},{9,8},{10,11... | collective-permute-start | bytes 589832 | tf_op jit(solution)/shard_map/ppermute | solution.py:34
  110.4 1.4 collective-permute-start.22
  127.2 1.2 collective-permute-start.25
  129.3 4.2 %collective-permute-start.26 = (bf16[32,768]{1,0:T(8,128)(2,1)S(1)}, bf16[32,768]{1,0:T(8,128)(2,1)S(1)}, u32[]{:S(2)}, u32[]{:S(2)}) collective-permute-start(bf16[32,768]{1,0:T(8,128)(2,1)S(1)} %add_convert_fusion.9), channel_id=1, source_target_pairs={{0,2},{1,3},{2,0},{3,1},{4,6},{5,7},{6,4},{7,5},{8,10},{9,11},{10,... | collective-permute-start | bytes 147464 | tf_op jit(solution)/shard_map/ppermute | solution.py:34
  133.5 4.2 %collective-permute-start.27 = (bf16[32,768]{1,0:T(8,128)(2,1)S(1)}, bf16[32,768]{1,0:T(8,128)(2,1)S(1)}, u32[]{:S(2)}, u32[]{:S(2)}) collective-permute-start(bf16[32,768]{1,0:T(8,128)(2,1)S(1)} %add_convert_fusion.8), channel_id=1, source_target_pairs={{0,4},{4,0},{8,12},{12,8},{16,20},{20,16},{24,28},{28,24},{1,5},{5... | collective-permute-start | bytes 147464 | tf_op jit(solution)/shard_map/ppermute | solution.py:34
  137.6 4.2 %collective-permute-start.28 = (bf16[32,768]{1,0:T(8,128)(2,1)S(1)}, bf16[32,768]{1,0:T(8,128)(2,1)S(1)}, u32[]{:S(2)}, u32[]{:S(2)}) collective-permute-start(bf16[32,768]{1,0:T(8,128)(2,1)S(1)} %add_convert_fusion.7), channel_id=1, source_target_pairs={{0,8},{4,12},{8,0},{12,4},{16,24},{20,28},{24,16},{28,20},{1,9},{5... | collective-permute-start | bytes 147464 | tf_op jit(solution)/shard_map/ppermute | solution.py:34
  141.8 10.9 %collective-permute-start.29 = (bf16[32,768]{1,0:T(8,128)(2,1)S(1)}, bf16[32,768]{1,0:T(8,128)(2,1)S(1)}, u32[]{:S(2)}, u32[]{:S(2)}) collective-permute-start(bf16[32,768]{1,0:T(8,128)(2,1)S(1)} %add_convert_fusion.6), channel_id=1, source_target_pairs={{0,16},{4,20},{8,24},{12,28},{16,0},{20,4},{24,8},{28,12},{1,17},{... | collective-permute-start | bytes 147464 | tf_op jit(solution)/shard_map/ppermute | solution.py:34
  150.7 8.7 %collective-permute-start.39 = (bf16[4,96,384]{2,1,0:T(8,128)(2,1)}, bf16[4,96,384]{2,1,0:T(8,128)(2,1)S(1)}, u32[]{:S(2)}, u32[]{:S(2)}) collective-permute-start(bf16[4,96,384]{2,1,0:T(8,128)(2,1)} %get-tuple-element.83), channel_id=1, source_target_pairs={{0,4},{4,0},{8,12},{12,8},{16,20},{20,16},{24,28},{28,24},{1,5},{5... | collective-permute-start | bytes 884744 | tf_op jit(solution)/shard_map/ppermute | solution.py:34
  151.2 11.5 %collective-permute-start.30 = (bf16[4,48,768]{2,1,0:T(8,128)(2,1)S(1)}, bf16[4,48,768]{2,1,0:T(8,128)(2,1)S(1)}, u32[]{:S(2)}, u32[]{:S(2)}) collective-permute-start(bf16[4,48,768]{2,1,0:T(8,128)(2,1)S(1)} %copy-done.38), channel_id=1, source_target_pairs={{0,4},{4,0},{8,12},{12,8},{16,20},{20,16},{24,28},{28,24},{1,5},{5... | collective-permute-start | bytes 884744 | tf_op jit(solution)/shard_map/ppermute | solution.py:34
  152.8 10.7 %collective-permute-start.23 = (bf16[256,768]{1,0:T(8,128)(2,1)}, bf16[256,768]{1,0:T(8,128)(2,1)S(1)}, u32[]{:S(2)}, u32[]{:S(2)}) collective-permute-start(bf16[256,768]{1,0:T(8,128)(2,1)} %get-tuple-element.77), channel_id=1, source_target_pairs={{0,1},{1,0},{2,3},{3,2},{4,5},{5,4},{6,7},{7,6},{8,9},{9,8},{10,11... | collective-permute-start | bytes 1179656 | tf_op jit(solution)/shard_map/ppermute | solution.py:34
  160.5 6.0 %collective-permute-start.40 = (bf16[2,96,384]{2,1,0:T(8,128)(2,1)S(1)}, bf16[2,96,384]{2,1,0:T(8,128)(2,1)S(1)}, u32[]{:S(2)}, u32[]{:S(2)}) collective-permute-start(bf16[2,96,384]{2,1,0:T(8,128)(2,1)S(1)} %slice.132), channel_id=1, source_target_pairs={{0,8},{4,12},{8,0},{12,4},{16,24},{20,28},{24,16},{28,20},{1,9},{5... | collective-permute-start | bytes 442376 | tf_op jit(solution)/shard_map/ppermute | solution.py:34
  162.7 6.3 %collective-permute-start.31 = (bf16[2,48,768]{2,1,0:T(8,128)(2,1)S(1)}, bf16[2,48,768]{2,1,0:T(8,128)(2,1)S(1)}, u32[]{:S(2)}, u32[]{:S(2)}) collective-permute-start(bf16[2,48,768]{2,1,0:T(8,128)(2,1)S(1)} %slice.122), channel_id=1, source_target_pairs={{0,8},{4,12},{8,0},{12,4},{16,24},{20,28},{24,16},{28,20},{1,9},{5... | collective-permute-start | bytes 442376 | tf_op jit(solution)/shard_map/ppermute | solution.py:34
  166.6 6.0 %collective-permute-start.41 = (bf16[1,96,384]{2,1,0:T(8,128)(2,1)S(1)}, bf16[1,96,384]{2,1,0:T(8,128)(2,1)S(1)}, u32[]{:S(2)}, u32[]{:S(2)}) collective-permute-start(bf16[1,96,384]{2,1,0:T(8,128)(2,1)S(1)} %slice.162), channel_id=1, source_target_pairs={{0,16},{4,20},{8,24},{12,28},{16,0},{20,4},{24,8},{28,12},{1,17},{... | collective-permute-start | bytes 221192 | tf_op jit(solution)/shard_map/ppermute | solution.py:34
  169.1 6.1 %collective-permute-start.32 = (bf16[1,48,768]{2,1,0:T(8,128)(2,1)S(1)}, bf16[1,48,768]{2,1,0:T(8,128)(2,1)S(1)}, u32[]{:S(2)}, u32[]{:S(2)}) collective-permute-start(bf16[1,48,768]{2,1,0:T(8,128)(2,1)S(1)} %slice.155), channel_id=1, source_target_pairs={{0,16},{4,20},{8,24},{12,28},{16,0},{20,4},{24,8},{28,12},{1,17},{... | collective-permute-start | bytes 221192 | tf_op jit(solution)/shard_map/ppermute | solution.py:34
  175.8 4.1 %collective-permute-start.35 = (bf16[24,192]{1,0:T(8,128)(2,1)S(1)}, bf16[24,192]{1,0:T(8,128)(2,1)S(1)}, u32[]{:S(2)}, u32[]{:S(2)}) collective-permute-start(bf16[24,192]{1,0:T(8,128)(2,1)S(1)} %get-tuple-element.112), channel_id=1, source_target_pairs={{0,3},{1,2},{2,1},{3,0},{4,7},{5,6},{6,5},{7,4},{8,11},{9,10},{10,... | collective-permute-start | bytes 27656 | tf_op jit(solution)/shard_map/ppermute | solution.py:34
  175.8 4.3 %collective-permute-start.34 = (bf16[24,192]{1,0:T(8,128)(2,1)S(1)}, bf16[24,192]{1,0:T(8,128)(2,1)S(1)}, u32[]{:S(2)}, u32[]{:S(2)}) collective-permute-start(bf16[24,192]{1,0:T(8,128)(2,1)S(1)} %get-tuple-element.113), channel_id=1, source_target_pairs={{0,2},{1,3},{2,0},{3,1},{4,6},{5,7},{6,4},{7,5},{8,10},{9,11},{10,... | collective-permute-start | bytes 27656 | tf_op jit(solution)/shard_map/ppermute | solution.py:34
  176.8 3.3 %collective-permute-start.33 = (bf16[24,192]{1,0:T(8,128)(2,1)S(1)}, bf16[24,192]{1,0:T(8,128)(2,1)S(1)}, u32[]{:S(2)}, u32[]{:S(2)}) collective-permute-start(bf16[24,192]{1,0:T(8,128)(2,1)S(1)} %get-tuple-element.114), channel_id=1, source_target_pairs={{0,1},{1,0},{2,3},{3,2},{4,5},{5,4},{6,7},{7,6},{8,9},{9,8},{10,11... | collective-permute-start | bytes 27656 | tf_op jit(solution)/shard_map/ppermute | solution.py:34
  178.3 5.9 %collective-permute-start.44 = (bf16[24,384]{1,0:T(8,128)(2,1)S(1)}, bf16[24,384]{1,0:T(8,128)(2,1)S(1)}, u32[]{:S(2)}, u32[]{:S(2)}) collective-permute-start(bf16[24,384]{1,0:T(8,128)(2,1)S(1)} %get-tuple-element.108), channel_id=1, source_target_pairs={{0,3},{1,2},{2,1},{3,0},{4,7},{5,6},{6,5},{7,4},{8,11},{9,10},{10,... | collective-permute-start | bytes 55304 | tf_op jit(solution)/shard_map/ppermute | solution.py:34
  178.9 5.3 %collective-permute-start.43 = (bf16[24,384]{1,0:T(8,128)(2,1)S(1)}, bf16[24,384]{1,0:T(8,128)(2,1)S(1)}, u32[]{:S(2)}, u32[]{:S(2)}) collective-permute-start(bf16[24,384]{1,0:T(8,128)(2,1)S(1)} %get-tuple-element.109), channel_id=1, source_target_pairs={{0,2},{1,3},{2,0},{3,1},{4,6},{5,7},{6,4},{7,5},{8,10},{9,11},{10,... | collective-permute-start | bytes 55304 | tf_op jit(solution)/shard_map/ppermute | solution.py:34
  179.9 4.3 %collective-permute-start.42 = (bf16[24,384]{1,0:T(8,128)(2,1)S(1)}, bf16[24,384]{1,0:T(8,128)(2,1)S(1)}, u32[]{:S(2)}, u32[]{:S(2)}) collective-permute-start(bf16[24,384]{1,0:T(8,128)(2,1)S(1)} %get-tuple-element.110), channel_id=1, source_target_pairs={{0,1},{1,0},{2,3},{3,2},{4,5},{5,4},{6,7},{7,6},{8,9},{9,8},{10,11... | collective-permute-start | bytes 55304 | tf_op jit(solution)/shard_map/ppermute | solution.py:34
  182.3 6.5 %collective-permute-start.36 = (bf16[1,48,768]{2,1,0:T(8,128)(2,1)}, bf16[1,48,768]{2,1,0:T(8,128)(2,1)S(1)}, u32[]{:S(2)}, u32[]{:S(2)}) collective-permute-start(bf16[1,48,768]{2,1,0:T(8,128)(2,1)} %bitcast.57), channel_id=1, source_target_pairs={{0,16},{4,20},{8,24},{12,28},{16,0},{20,4},{24,8},{28,12},{1,17},{... | collective-permute-start | bytes 221192 | tf_op jit(solution)/shard_map/ppermute | solution.py:34
  183.1 11.5 %collective-permute-start.24 = (bf16[128,768]{1,0:T(8,128)(2,1)S(1)}, bf16[128,768]{1,0:T(8,128)(2,1)S(1)}, u32[]{:S(2)}, u32[]{:S(2)}) collective-permute-start(bf16[128,768]{1,0:T(8,128)(2,1)S(1)} %fusion.7), channel_id=1, source_target_pairs={{0,2},{1,3},{2,0},{3,1},{4,6},{5,7},{6,4},{7,5},{8,10},{9,11},{10,... | collective-permute-start | bytes 589832 | tf_op jit(solution)/shard_map/ppermute | solution.py:34
  186.4 7.1 %collective-permute-start.45 = (bf16[1,48,768]{2,1,0:T(8,128)(2,1)}, bf16[1,48,768]{2,1,0:T(8,128)(2,1)S(1)}, u32[]{:S(2)}, u32[]{:S(2)}) collective-permute-start(bf16[1,48,768]{2,1,0:T(8,128)(2,1)} %bitcast.59), channel_id=1, source_target_pairs={{0,16},{4,20},{8,24},{12,28},{16,0},{20,4},{24,8},{28,12},{1,17},{... | collective-permute-start | bytes 221192 | tf_op jit(solution)/shard_map/ppermute | solution.py:34
  189.7 6.9 %collective-permute-start.37 = (bf16[2,48,768]{2,1,0:T(8,128)(2,1)S(1)}, bf16[2,48,768]{2,1,0:T(8,128)(2,1)S(1)}, u32[]{:S(2)}, u32[]{:S(2)}) collective-permute-start(bf16[2,48,768]{2,1,0:T(8,128)(2,1)S(1)} %get-tuple-element.105), channel_id=1, source_target_pairs={{0,8},{4,12},{8,0},{12,4},{16,24},{20,28},{24,16},{28,20},{1,9},{5... | collective-permute-start | bytes 442376 | tf_op jit(solution)/shard_map/ppermute | solution.py:34
  194.4 5.2 %collective-permute-start.46 = (bf16[2,48,768]{2,1,0:T(8,128)(2,1)S(1)}, bf16[2,48,768]{2,1,0:T(8,128)(2,1)S(1)}, u32[]{:S(2)}, u32[]{:S(2)}) collective-permute-start(bf16[2,48,768]{2,1,0:T(8,128)(2,1)S(1)} %get-tuple-element.103), channel_id=1, source_target_pairs={{0,8},{4,12},{8,0},{12,4},{16,24},{20,28},{24,16},{28,20},{1,9},{5... | collective-permute-start | bytes 442376 | tf_op jit(solution)/shard_map/ppermute | solution.py:34
  196.7 9.9 %collective-permute-start.38 = (bf16[4,48,768]{2,1,0:T(8,128)(2,1)S(1)}, bf16[4,48,768]{2,1,0:T(8,128)(2,1)S(1)}, u32[]{:S(2)}, u32[]{:S(2)}) collective-permute-start(bf16[4,48,768]{2,1,0:T(8,128)(2,1)S(1)} %bitcast.51), channel_id=1, source_target_pairs={{0,4},{4,0},{8,12},{12,8},{16,20},{20,16},{24,28},{28,24},{1,5},{5... | collective-permute-start | bytes 884744 | tf_op jit(solution)/shard_map/ppermute | solution.py:34
  199.7 11.0 %collective-permute-start.47 = (bf16[4,48,768]{2,1,0:T(8,128)(2,1)S(1)}, bf16[4,48,768]{2,1,0:T(8,128)(2,1)S(1)}, u32[]{:S(2)}, u32[]{:S(2)}) collective-permute-start(bf16[4,48,768]{2,1,0:T(8,128)(2,1)S(1)} %bitcast.53), channel_id=1, source_target_pairs={{0,4},{4,0},{8,12},{12,8},{16,20},{20,16},{24,28},{28,24},{1,5},{5... | collective-permute-start | bytes 884744 | tf_op jit(solution)/shard_map/ppermute | solution.py:34
  (39 other events, 379.9 us)
where the time goes:
time: 215 us; the launch traced here: 214 us
  waiting for transfers between devices  75.3 us (35%)
  Pallas kernels  52.5 us (24%)
  starting transfers between devices  34.8 us (16%)
  blocking collectives  25.6 us (12%)
  local copies, waits for them, and re-layouts  13.5 us (6%)
  other arithmetic  11.2 us (5%)
    ppermute x48, waiting for transfers between devices, exchange(): return lax.ppermute(value, axis, [(i, i ^ mask) for i in range(size)])  75.3 us
    pallas_call x9, Pallas kernels, call_whole(): pl.pallas_call(kernel, out_shape=[jax.ShapeDtypeStruct(s, d) for s, d in...  38.2 us
    ppermute x48, starting transfers between devices, exchange(): return lax.ppermute(value, axis, [(i, i ^ mask) for i in range(size)])  34.8 us
    all_to_all x1, blocking collectives, body(): lax.all_to_all(send.reshape(size, local * CAP, 2 * width), 'expert', 0, 0...  14 us
    all_to_all x1, blocking collectives, body(): lax.all_to_all(returned.reshape(size, local * CAP, 2 * width), 'expert',...  11.6 us
    pallas_call x1, Pallas kernels, body(): grad_expert_in, grad_expert_out = weights_call(*xs, hidden, gpre)  7.49 us
    pallas_call x1, Pallas kernels, body(): pl.pallas_call(lambda *r: experts_kernel(groups, local, *r), grid=(steps,...  6.82 us
    unnamed x80, local copies, waits for them, and re-layouts  6.21 us
  transfers between devices with their start and end apart: 48, of which 27 were waited for; matrix products, arithmetic and copies ran while one was open for 7% of the time, Pallas kernels for 10%

commit v1 on v0

--- a/solution.py
+++ b/solution.py
@@ -100,9 +100,13 @@
     third = w_ref.shape[1] // 3
     part = third // groups
     for d in range(groups):
-        for s in range(3):
-            chunks[d, :, s * part : (s + 1) * part] = w_ref[
+        for s in range(2):
+            chunks[d, 0:part, s * part : (s + 1) * part] = w_ref[
                 :, s * third + d * part : s * third + (d + 1) * part
+            ]
+        for s in range(2):
+            chunks[d, part:, s * part : (s + 1) * part] = w_ref[
+                s * part // 2 : (s + 1) * part // 2, 2 * third + d * part : 2 * third + (d + 1) * part
             ]
     for k in range(groups):
         outs[k][...] = chunks[me ^ k]
@@ -132,7 +136,7 @@
     tab_ref = outs[5 + groups]
     me = me_ref[0]
     count = tok[0].shape[0]
-    wrows = wp[0].shape[0]
+    wrows = wp[0].shape[0] * 2 // 3
     length = count * groups
     extra = sum_refs(ext)
     gain = extra[12:13, :]
@@ -140,7 +144,12 @@
     for k in range(groups):
         x = tok[k][...].astype(F32)
         normed_ref[rows_at(me ^ k, count), :] = (x * norm_scale(x) * gain).astype(BF16)
-        wfull_ref[rows_at(me ^ k, wrows), :] = wp[k][...]
+        cols = 2 * heads * hs
+        wfull_ref[rows_at(me ^ k, wrows), :cols] = wp[k][:wrows, :]
+        for s in range(2):
+            wfull_ref[rows_at(2 * (me ^ k) + s, wrows // 2), cols:] = wp[k][
+                wrows:, s * cols // 2 : (s + 1) * cols // 2
+            ]
     proj_ref[...] = dot_nn(normed_ref[...], wfull_ref[...]).astype(BF16)
     distance = distance_tile()
     factor = hs ** (-0.5)
@@ -381,23 +390,16 @@
 
 
 def scores_kernel(groups, heads, hs, slots, me_ref, *refs):
-    tok = refs[:groups]
-    gm_ref, gv_ref, proj_ref, prob_ref, normed_ref, wfull_ref = refs[groups : groups + 6]
-    early_ref = refs[groups + 6]
-    outs = refs[groups + 7 :]
-    send_ref, keep_ref, rows_ref, own_ref, mid_ref, small_ref = outs[:6]
-    gproj_ref, gi_ref, gn_ref = outs[6:]
+    gm_ref, gv_ref, proj_ref, prob_ref, normed_ref = refs[:5]
+    send_ref, keep_ref, gproj_ref, tiles_ref, gi_ref = refs[5:]
     me = me_ref[0]
     pos = me_ref[1]
-    count, width = tok[0].shape
-    length = count * groups
+    length, width = normed_ref.shape
     factor = hs ** (-0.5)
     part = heads * hs
     blocks_n = length // BLOCK
-    distance = distance_tile()
     dqs = [[None] * heads for _ in range(blocks_n)]
     dks = [[None] * heads for _ in range(blocks_n)]
-    tiles = []
     for h in range(heads):
         near = jnp.zeros((BLOCK, BLOCK), F32)
         prev = jnp.zeros((BLOCK, BLOCK), F32)
@@ -427,7 +429,7 @@
                     dks[kb][h] = dk[cut]
                 else:
                     dks[kb][h] = dks[kb][h] + dk[cut]
-        tiles.append((jnp.concatenate([prev, near], axis=1), rest))
+        tiles_ref[h] = jnp.concatenate([prev, near, rest], axis=1)
     for b in range(blocks_n):
         span = slice(b * BLOCK, (b + 1) * BLOCK)
         full = jnp.concatenate(dqs[b] + [d * factor for d in dks[b]], axis=1)
@@ -447,6 +449,15 @@
                 send_ref[s // 2] = both
             else:
                 keep_ref[s // 2] = both
+
+
+def rest_kernel(groups, heads, me_ref, *refs):
+    tok = refs[:groups]
+    gproj_ref, wfull_ref, tiles_ref, early_ref = refs[groups : groups + 4]
+    rows_ref, own_ref, mid_ref, small_ref, gn_ref = refs[groups + 4 :]
+    me = me_ref[0]
+    count, width = tok[0].shape
+    distance = distance_tile()
     gn_ref[...] = dot_nt(gproj_ref[...], wfull_ref[...])
     total = jnp.zeros((1, width), F32)
     for k in range(groups):
@@ -464,8 +475,8 @@
     small_ref[...] = early_ref[...]
     small_ref[12:13, :] = total
     for h in range(heads):
-        tile, rest = tiles[h]
-        far = jnp.sum(rest, axis=0, keepdims=True)
+        tile = tiles_ref[h, :, : 2 * BLOCK]
+        far = jnp.sum(tiles_ref[h, :, 2 * BLOCK :], axis=0, keepdims=True)
         far = jnp.concatenate([far, jnp.zeros_like(far)], axis=1)
         sums = []
         for n in range(NB):
@@ -477,7 +488,12 @@
         sums = jnp.transpose(jnp.concatenate(sums, axis=0))
         line = jnp.sum(sums, axis=0, keepdims=True)
         index = lax.broadcasted_iota(jnp.int32, (16, NB), 0)
-        small_ref[0:16, 0:NB] += jnp.where(index == me * heads + h, line, 0.0)
+        placed = jnp.where(index == me * heads + h, line, 0.0)
+        per = NB // groups
+        for w in range(groups):
+            at = w * (width // groups)
+            small_ref[0:16, at : at + per] += placed[:, w * per : (w + 1) * per]
+    rows_ref[2 * count :, :] = small_ref[...].astype(BF16)
 
 
 def natural(pieces, me):
@@ -492,14 +508,13 @@
 
 def join_kernel(groups, me_ref, *refs):
     pieces = [r[...].astype(F32) for r in refs[:groups]]
-    rest = refs[groups:-1]
+    own_ref, rider_ref, first_ref, second_ref = refs[groups:]
     me = me_ref[0]
-    if rest:
-        both = [rest[0][...].astype(F32), natural(pieces, me)]
-    else:
-        half = pieces[0].shape[1] // 2
-        both = [natural([p[:, i * half : (i + 1) * half] for p in pieces], me) for i in range(2)]
-    refs[-1][...] = jnp.concatenate(both, axis=0).astype(BF16)
+    part = pieces[0].shape[1] // 3
+    q, k, v = [natural([p[:, i * part : (i + 1) * part] for p in pieces], me) for i in range(3)]
+    first = jnp.concatenate([own_ref[...].astype(F32), v, rider_ref[...]], axis=0)
+    first_ref[...] = first.astype(BF16)
+    second_ref[...] = jnp.concatenate([q, k], axis=0).astype(BF16)
 
 
 def final_kernel(slots, me_ref, *refs):
@@ -511,8 +526,9 @@
     third = out_ref.shape[1] // 3
     for s in range(slots):
         target = pl.ds(pl.multiple_of((pos ^ s) * rows, 8), rows)
-        one = first[s % 2][s // 2].astype(F32)
-        two = second[s % 2][s // 2].astype(F32)
+        at = [spread_place(s, spread_bits(slots, swap)) * 2 * rows for swap in (False, True)]
+        one = first[s % 2][at[0] : at[0] + 2 * rows, :].astype(F32)
+        two = second[s % 2][at[1] : at[1] + 2 * rows, :].astype(F32)
         own_ref[target, :] = one[:rows]
         out_ref[target, 2 * third :] = one[rows:]
         out_ref[target, :third] = two[:rows]
@@ -531,24 +547,41 @@
         bit *= 2
 
 
-def spread_slots(value, axis):
-    bit = lax.axis_size(axis) // 2
+def spread_bits(size, swap=False):
+    bits = []
+    bit = size // 2
+    while bit >= 1:
+        bits.append(bit)
+        bit //= 2
+    if swap and len(bits) > 2:
+        bits[0], bits[1] = bits[1], bits[0]
+    return bits
+
+
+def spread_place(s, bits):
+    place = 0
+    for bit in bits[:-1]:
+        place = 2 * place + (1 if s & bit else 0)
+    return place
+
+
+def spread_slots(value, rows, axis, bits):
+    width = value.shape[1]
+    slots = 1
     while True:
+        bit = bits[slots.bit_length() - 1]
         got = exchange(value, axis, bit)
-        if bit == 1:
-            return value, got
-        value = jnp.stack([value, got], axis=1).reshape((-1,) + value.shape[1:])
-        bit //= 2
-
-
-def sum_all(value, axes):
-    for axis in axes:
-        bit = 1
-        while bit < lax.axis_size(axis):
-            sent = value.astype(BF16)
-            value = sent.astype(F32) + exchange(sent, axis, bit).astype(F32)
-            bit *= 2
-    return value
+        end = slots * rows
+        rider = None
+        if value.shape[0] > end:
+            rider = value[end:].astype(F32) + got[end:].astype(F32)
+        if bit == bits[-1]:
+            return (value, got), rider
+        pair = [v[:end].reshape(slots, rows, width) for v in (value, got)]
+        value = jnp.stack(pair, axis=1).reshape(2 * end, width)
+        if rider is not None:
+            value = jnp.concatenate([value, rider.astype(BF16)], axis=0)
+        slots *= 2
 
 
 def reduce_rows(send, keep, mid, axis):
@@ -604,10 +637,10 @@
     tok = gather_xor(tokens, "wshard")
     chunks = whole(
         lambda *r: prepare_kernel(groups, *r),
-        [((part, 3 * part), BF16)] * groups,
+        [((3 * part // 2, 2 * part), BF16)] * groups,
         where,
         proj_inputs,
-        scratch=[pltpu.VMEM((groups, part, 3 * part), BF16)],
+        scratch=[pltpu.VMEM((groups, 3 * part // 2, 2 * part), BF16)],
     )
     wp = [chunks[0]] + [exchange(chunks[k], "wshard", k) for k in range(1, groups)]
     ext = gather_xor(small, "wshard")
@@ -754,31 +787,40 @@
             pltpu.VMEM((width, part), F32),
         ],
     )
-    second_send, second_keep, gn_send, gn_keep, gn_mid, sums = whole(
+    second_send, second_keep, gproj, tiles = whole(
         lambda *r: scores_kernel(groups, heads, hs, cuts, *r),
         second_shapes
-        + [
-            ((2 * count, width), BF16),
-            ((count, width), F32),
-            ((count, width), F32),
-            ((experts + 16, width), F32),
-        ],
+        + [((length, 3 * part), BF16), ((heads, BLOCK, 3 * BLOCK), F32)],
         where,
-        *tok,
         gm,
         gv,
         projected,
         prob,
         normed_one,
+        scratch=[pltpu.VMEM((width, 2 * part), F32)],
+    )
+    gn_send, gn_keep, gn_mid, sums = whole(
+        lambda *r: rest_kernel(groups, heads, *r),
+        [
+            ((2 * count + experts + 16, width), BF16),
+            ((count, width), F32),
+            ((count, width), F32),
+            ((experts + 16, width), F32),
+        ],
+        where,
+        *tok,
+        gproj,
         wfull,
+        tiles,
         early,
-        scratch=[
-            pltpu.VMEM((length, 3 * part), BF16),
-            pltpu.VMEM((width, 2 * part), F32),
-            pltpu.VMEM((length, width), F32),
-        ],
-    )
-    grad_normed_one = reduce_rows(gn_send, gn_keep, gn_mid, "wshard")
+        scratch=[pltpu.VMEM((length, width), F32)],
+    )
+    got = exchange(gn_send, "wshard", 1).astype(F32)
+    sums = sums + got[2 * count :]
+    other = jnp.concatenate([gn_mid + got[count : 2 * count], sums], axis=0).astype(BF16)
+    other = exchange(other, "wshard", 2).astype(F32)
+    grad_normed_one = gn_keep + got[:count] + other[:count]
+    sums = sums + other[count:]
     inputs = tokens.astype(F32)
     scale_one = norm_scale(inputs)
     gain_one_f = sum(e[12:13].astype(F32) for e in ext)
@@ -788,32 +830,30 @@
         scale_one * scaled - inputs * scale_one * scale_one * scale_one * inner
     )
 
-    sums = sum_all(sums, ("wshard", "expert"))
-    grad_router = lax.dynamic_slice(sums[16:], (0, me * part), (experts, part)).T
-    grad_gain_two = lax.dynamic_slice(sums[13], (me * part,), (part,))
-    grad_gain_one = lax.dynamic_slice(sums[12], (me * part,), (part,))
-    per = buckets // groups
-    grad_table = lax.dynamic_slice(sums, (0, me * per), (heads_all, per)).T
+    lines = experts + 16
+    sums = lax.dynamic_slice(sums, (0, me * part), (lines, part))
 
     if fast:
         one = reduce_slots(first_send, first_keep, "expert").astype(BF16)
-        cut = [one[step:, t * part : (t + 1) * part] for t in range(groups)]
+        two = reduce_slots(second_send, second_keep, "expert").astype(BF16)
+        cut = [
+            jnp.concatenate(
+                [two[t * step : (t + 1) * step], one[step:, t * part : (t + 1) * part]], axis=1
+            )
+            for t in range(groups)
+        ]
         cut = [cut[0]] + [exchange(cut[t], "wshard", t) for t in range(1, groups)]
-        one = whole(
+        one, two = whole(
             lambda *r: join_kernel(groups, *r),
-            [((2 * step, width), BF16)],
+            [((2 * step + lines // groups, width), BF16), ((2 * step, width), BF16)],
             where,
             *cut,
             one[:step],
-        )[0]
-        one = spread_slots(one[None], "expert")
-        two = reduce_slots(second_send, second_keep, "expert").astype(BF16)
-        cut = [two[t * step : (t + 1) * step] for t in range(groups)]
-        cut = [cut[0]] + [exchange(cut[t], "wshard", t) for t in range(1, groups)]
-        two = whole(
-            lambda *r: join_kernel(groups, *r), [((2 * step, width), BF16)], where, *cut
-        )[0]
-        two = spread_slots(two[None], "expert")
+            sums.reshape(lines // groups, width),
+        )
+        one, sums = spread_slots(one, 2 * step, "expert", spread_bits(size))
+        sums = sums.reshape(lines, part)
+        two, _ = spread_slots(two, 2 * step, "expert", spread_bits(size, True))
         total_inputs, total_output = whole(
             lambda *r: final_kernel(size, *r),
             [((part, 3 * width), F32), ((part, width), F32)],
@@ -822,11 +862,16 @@
             *two,
         )
     else:
+        sums = lax.psum(sums, "expert")
         total_output = lax.psum(first_send.astype(F32), "expert")
         total = jnp.concatenate([second_send, first_keep], axis=1)
         total = lax.psum(total, "expert").reshape(groups, part, 3, part)
         total = lax.all_to_all(total, "wshard", 0, 0, tiled=True)
         total_inputs = total.transpose(1, 2, 0, 3).reshape(part, 3 * width).astype(F32)
+    grad_router = sums[16:].T
+    grad_gain_two = sums[13]
+    grad_gain_one = sums[12]
+    grad_table = sums[:heads_all, : buckets // groups].T
     return (
         output,
         grad_tokens,

time: 215 us -> 195 us (0.907)
  waiting for transfers between devices: 75.3 us -> 62.6 us
  starting transfers between devices: 34.8 us -> 28.9 us
  other arithmetic: 11.2 us -> 8.14 us
    ppermute x48 -> x40, waiting for transfers between devices: 75.3 us -> 62.6 us  [exchange(): return lax.ppermute(value, axis, [(i, i ^ mask) for i in range(size)])]
    ppermute x48 -> x40, starting transfers between devices: 34.8 us -> 28.9 us  [exchange(): return lax.ppermute(value, axis, [(i, i ^ mask) for i in range(size)])]
    another operation x8 -> x10, other arithmetic: 3.05 us -> 0.39 us  [the longest x4 1.87 us: spread_slots(): value = jnp.stack([value, got], axis=1).reshape((-1,) + value.shape[1:])]
  transfers between devices with their start and end apart: 48 -> 40, of which waited for: 27 -> 22; matrix products, arithmetic and copies ran while one was open for 7% -> 8% of each run, Pallas kernels for 10% -> 12%
where the time goes in v1:
time: 195 us; the launch traced here: 194 us
  waiting for transfers between devices  62.6 us (32%)
  Pallas kernels  54.3 us (28%)
  starting transfers between devices  28.9 us (15%)
  blocking collectives  25.6 us (13%)
  local copies, waits for them, and re-layouts  13.5 us (7%)
  other arithmetic  8.14 us (4%)
    ppermute x40, waiting for transfers between devices, exchange(): return lax.ppermute(value, axis, [(i, i ^ mask) for i in range(size)])  62.6 us
    pallas_call x9, Pallas kernels, call_whole(): pl.pallas_call(kernel, out_shape=[jax.ShapeDtypeStruct(s, d) for s, d in...  40 us
    ppermute x40, starting transfers between devices, exchange(): return lax.ppermute(value, axis, [(i, i ^ mask) for i in range(size)])  28.9 us
    all_to_all x1, blocking collectives, body(): lax.all_to_all(send.reshape(size, local * CAP, 2 * width), 'expert', 0, 0...  14 us
    all_to_all x1, blocking collectives, body(): lax.all_to_all(returned.reshape(size, local * CAP, 2 * width), 'expert',...  11.6 us
    pallas_call x1, Pallas kernels, body(): grad_expert_in, grad_expert_out = weights_call(*xs, hidden, gpre)  7.49 us
    pallas_call x1, Pallas kernels, body(): pl.pallas_call(lambda *r: experts_kernel(groups, local, *r), grid=(steps,...  6.81 us
    unnamed x80, local copies, waits for them, and re-layouts  5.73 us
  transfers between devices with their start and end apart: 40, of which 22 were waited for; matrix products, arithmetic and copies ran while one was open for 8% of the time, Pallas kernels for 12%

profile of v1, /device:TPU:0, one launch (start us, length us, event | category | flops | bytes accessed | tf_op | source)
XLA Modules:
  0.0 194.2 jit_solution(3518441364009786923)
XLA Ops:
  0.6 3.0 %collective-permute-start.4 = (bf16[128,768]{1,0:T(8,128)(2,1)}, bf16[128,768]{1,0:T(8,128)(2,1)S(1)}, u32[]{:S(2)}, u32[]{:S(2)}) collective-permute-start(bf16[128,768]{1,0:T(8,128)(2,1)} %r_1_.5), channel_id=1, source_target_pairs={{0,2},{1,3},{2,0},{3,1},{4,6},{5,7},{6,4},{7,5},{8,10},{9,11},{10,... | collective-permute-start | bytes 589832 | tf_op jit(solution)/shard_map/ppermute | solution.py:34
  6.7 1.7 dynamic_update_slice.11.r_9_.r_8_.r_0_
  9.2 1.8 collective-permute-start.13
  11.7 2.3 %shard_map.204 = (bf16[288,384]{1,0:T(8,128)(2,1)}, bf16[288,384]{1,0:T(8,128)(2,1)}, bf16[288,384]{1,0:T(8,128)(2,1)}, bf16[288,384]{1,0:T(8,128)(2,1)}) custom-call(s32[2]{0:T(128)} %pad_add_fusion.r_0_, bf16[192,2304]{1,0:T(8,128)(2,1)} %r_1_.3), custom_call_target="tpu_custom_call" | custom-call | tf_op jit(solution)/shard_map/pallas_call | solution.py:54
  14.5 1.2 collective-permute-done.2.r_12_.r_11_.r_3_
  16.0 1.3 collective-permute-start.8
  19.1 5.2 %collective-permute-done.7.r_7_ = bf16[288,384]{1,0:T(8,128)(2,1)S(1)} collective-permute-done((bf16[288,384]{1,0:T(8,128)(2,1)}, bf16[288,384]{1,0:T(8,128)(2,1)S(1)}, u32[]{:S(2)}, u32[]{:S(2)}) %collective-permute-start.7) | collective-permute-done | bytes 221216 | tf_op jit(solution)/shard_map/ppermute | solution.py:34
  24.3 3.4 %collective-permute-done.8.r_8_ = bf16[288,384]{1,0:T(8,128)(2,1)S(1)} collective-permute-done((bf16[288,384]{1,0:T(8,128)(2,1)}, bf16[288,384]{1,0:T(8,128)(2,1)S(1)}, u32[]{:S(2)}, u32[]{:S(2)}) %collective-permute-start.8) | collective-permute-done | bytes 221216 | tf_op jit(solution)/shard_map/ppermute | solution.py:34
  28.5 9.4 %shard_map.205 = (bf16[512,768]{1,0:T(8,128)(2,1)}, bf16[768,576]{1,0:T(8,128)(2,1)}, bf16[512,576]{1,0:T(8,128)(2,1)}, bf16[512,192]{1,0:T(8,128)(2,1)}, f32[3,...) custom-call(s32[2]{0:T(128)} %pad_add_fusion.r_0_, ...), custom_call_target="tpu_custom_call" | custom-call | tf_op jit(solution)/shard_map/pallas_call | solution.py:54
  38.4 1.3 collective-permute-start.10
  39.8 1.4 add_convert_fusion.8.r_14_.r_9_
  41.2 1.7 collective-permute-done.10.r_2_
  42.9 1.4 collective-permute-done.11.r_3_
  45.1 3.4 %shard_map.206 = (f32[128,768]{1,0:T(8,128)}, bf16[128,768]{1,0:T(8,128)(2,1)}, bf16[64,1536]{1,0:T(8,128)(2,1)}, f32[128,128]{1,0:T(8,128)}) custom-call(bf16[128,192]{1,0:T(8,128)(2,1)} %get-tuple-element.58.r_0_, bf16[128,192]{1,0:T(8,128)(2,1)} %copy-done.32, bf16[128,192]{1,0:T(8,128)(2,1)} %copy-done.33, bf16[128,192]{1,0:T(8,128)(2,1)} %copy-done.34, ...), custom_call_target="tpu_custom_call" | custom-call | tf_op jit(solution)/shard_map/pallas_call | solution.py:54
  48.5 14.0 %all_to_all.10 = bf16[8,8,1536]{2,1,0:T(8,128)(2,1)S(1)} all-to-all(bf16[8,8,1536]{2,1,0:T(8,128)(2,1)} %bitcast.54), channel_id=1, replica_groups=mesh['expert'=8,'wshard'=4] {'expert'}, dimensions={0} | all-to-all | bytes 393216 | tf_op jit(solution)/shard_map/all_to_all | solution.py:686
  63.6 4.6 %collective-permute-done.16.r_2_ = bf16[64,1536]{1,0:T(8,128)(2,1)S(1)} collective-permute-done((bf16[64,1536]{1,0:T(8,128)(2,1)S(1)}, bf16[64,1536]{1,0:T(8,128)(2,1)S(1)}, u32[]{:S(2)}, u32[]{:S(2)}) %collective-permute-start.16) | collective-permute-done | bytes 196640 | tf_op jit(solution)/shard_map/ppermute | solution.py:34
  68.2 1.4 collective-permute-done.17.r_3_
  70.3 6.8 %shard_map.207 = (bf16[256,768]{1,0:T(8,128)(2,1)}, bf16[256,768]{1,0:T(8,128)(2,1)}, bf16[128,1536]{1,0:T(8,128)(2,1)}, f32[64,1536]{1,0:T(8,128)}, f32[64,1536]{1,0:T(8,128)}) custom-call(bf16[64,1536]{1,0:T(8,128)(2,1)} %bitcast.45, bf16[64,1536]{1,0:T(8,128)(2,1)} %copy-done.6, bf16[64,1536]{1,0:T(8,128)(2,1)} %copy-done.5, bf16[64,1536]{1,0:T(8,128)(2,1)} %copy-done.7, ...), custom_call_target="tpu_custom_call" | custom-call | tf_op jit(solution)/shard_map/pallas_call | solution.py:695
  77.3 1.8 collective-permute-done.18
  79.2 1.1 fusion.9
  80.3 1.1 collective-permute-start.19
  81.4 5.9 %collective-permute-done.19 = bf16[64,1536]{1,0:T(8,128)(2,1)S(1)} collective-permute-done((bf16[64,1536]{1,0:T(8,128)(2,1)S(1)}, bf16[64,1536]{1,0:T(8,128)(2,1)S(1)}, u32[]{:S(2)}, u32[]{:S(2)}) %collective-permute-start.19) | collective-permute-done | bytes 196640 | tf_op jit(solution)/shard_map/ppermute | solution.py:34
  87.3 1.1 fusion.12
  88.3 11.6 %all_to_all.11 = bf16[8,8,1536]{2,1,0:T(8,128)(2,1)} all-to-all(bf16[8,8,1536]{2,1,0:T(8,128)(2,1)S(1)} %fusion.12), channel_id=1, replica_groups=mesh['expert'=8,'wshard'=4] {'expert'}, dimensions={0} | all-to-all | bytes 393216 | tf_op jit(solution)/shard_map/all_to_all | solution.py:745
  99.9 3.6 %shard_map.208 = (bf16[128,768]{1,0:T(8,128)(2,1)}, f32[128,768]{1,0:T(8,128)}, bf16[128,768]{1,0:T(8,128)(2,1)}, f32[32,768]{1,0:T(8,128)}) custom-call(bf16[32,768]{1,0:T(8,128)(2,1)} %copy-done.4, bf16[32,768]{1,0:T(8,128)(2,1)} %copy-done.12, bf16[32,768]{1,0:T(8,128)(2,1)} %copy-done.11, bf16[32,768]{1,0:T(8,128)(2,1)} %copy-done.13, ...), custom_call_target="tpu_custom_call" | custom-call | tf_op jit(solution)/shard_map/pallas_call | solution.py:54
  104.5 4.8 %collective-permute-done.21.r_3_ = bf16[128,768]{1,0:T(8,128)(2,1)S(1)} collective-permute-done((bf16[128,768]{1,0:T(8,128)(2,1)}, bf16[128,768]{1,0:T(8,128)(2,1)S(1)}, u32[]{:S(2)}, u32[]{:S(2)}) %collective-permute-start.21) | collective-permute-done | bytes 196640 | tf_op jit(solution)/shard_map/ppermute | solution.py:34
  109.4 1.4 collective-permute-done.22.r_4_
  111.5 5.2 %shard_map.209 = (bf16[512,192]{1,0:T(8,128)(2,1)}, bf16[512,192]{1,0:T(8,128)(2,1)}, bf16[4,48,768]{2,1,0:T(8,128)(2,1)}, bf16[4,48,768]{2,1,0:T(8,128)(2,1)}) custom-call(s32[2]{0:T(128)} %pad_add_fusion.r_0_, bf16[128,768]{1,0:T(8,128)(2,1)} %get-tuple-element.71.r_1_, bf16[128,768]{1,0:T(8,128)(2,1)} %copy-done.28, bf16[128,768]{1,0:T(8,128)(2,1)} %copy-done.27, ...), custom_call_target="tpu_custom_call" | custom-call | tf_op jit(solution)/shard_map/pallas_call | solution.py:54
  116.6 6.9 %shard_map.210 = (bf16[4,96,384]{2,1,0:T(8,128)(2,1)}, bf16[4,96,384]{2,1,0:T(8,128)(2,1)}, bf16[512,576]{1,0:T(8,128)(2,1)}, f32[3,128,384]{2,1,0:T(8,128)}) custom-call(s32[2]{0:T(128)} %pad_add_fusion.r_0_, bf16[512,192]{1,0:T(8,128)(2,1)} %get-tuple-element.75.r_1_, bf16[512,192]{1,0:T(8,128)(2,1)} %get-tuple-element.76.r_2_, ...), custom_call_target="tpu_custom_call" | custom-call | tf_op jit(solution)/shard_map/pallas_call | solution.py:54
  124.6 1.1 collective-permute-start.28
  126.4 7.5 %shard_map.214 = (f32[2,768,768]{2,1,0:T(8,128)}, f32[2,768,768]{2,1,0:T(8,128)}) custom-call(bf16[64,1536]{1,0:T(8,128)(2,1)} %bitcast.46, bf16[64,1536]{1,0:T(8,128)(2,1)} %copy-done.6, bf16[64,1536]{1,0:T(8,128)(2,1)} %copy-done.5, bf16[64,1536]{1,0:T(8,128)(2,1)} %copy-done.7, bf16[256,768]{1,0:T(8,128)(2,1)} %get-tuple-element.94.r_4_, ...), custom_call_target="tpu_custom_call" | custom-call | tf_op jit(solution)/shard_map/pallas_call | solution.py:742
  133.9 4.9 %shard_map.211 = (bf16[288,768]{1,0:T(8,128)(2,1)}, f32[128,768]{1,0:T(8,128)}, f32[128,768]{1,0:T(8,128)}, f32[32,768]{1,0:T(8,128)}) custom-call(s32[2]{0:T(128)} %pad_add_fusion.r_0_, bf16[128,768]{1,0:T(8,128)(2,1)} %r_1_.5, bf16[128,768]{1,0:T(8,128)(2,1)} %copy-done.9, bf16[128,768]{1,0:T(8,128)(2,1)} %copy-done.8, bf16[128,768]{1,0:T(8,128)(2,1)} %copy-done.10, ...), custom_call_target="tpu_custom_call" | custom-call | tf_op jit(solution)/shard_map/pallas_call | solution.py:54
  139.3 1.9 collective-permute-start.29
  141.3 4.5 %collective-permute-done.26 = bf16[2,96,384]{2,1,0:T(8,128)(2,1)S(1)} collective-permute-done((bf16[2,96,384]{2,1,0:T(8,128)(2,1)S(1)}, bf16[2,96,384]{2,1,0:T(8,128)(2,1)S(1)}, u32[]{:S(2)}, u32[]{:S(2)}) %collective-permute-start.26) | collective-permute-done | bytes 147488 | tf_op jit(solution)/shard_map/ppermute | solution.py:34
  146.5 1.9 %collective-permute-done.29 = bf16[2,48,768]{2,1,0:T(8,128)(2,1)S(1)} collective-permute-done((bf16[2,48,768]{2,1,0:T(8,128)(2,1)S(1)}, bf16[2,48,768]{2,1,0:T(8,128)(2,1)S(1)}, u32[]{:S(2)}, u32[]{:S(2)}) %collective-permute-start.29) | collective-permute-done | bytes 147488 | tf_op jit(solution)/shard_map/ppermute | solution.py:34
  149.4 1.1 collective-permute-start.24
  150.5 1.1 collective-permute-done.27
  151.7 3.1 %collective-permute-done.30 = bf16[1,48,768]{2,1,0:T(8,128)(2,1)S(1)} collective-permute-done((bf16[1,48,768]{2,1,0:T(8,128)(2,1)S(1)}, bf16[1,48,768]{2,1,0:T(8,128)(2,1)S(1)}, u32[]{:S(2)}, u32[]{:S(2)}) %collective-permute-start.30) | collective-permute-done | bytes 73760 | tf_op jit(solution)/shard_map/ppermute | solution.py:34
  155.0 1.1 collective-permute-start.32
  160.2 1.6 shard_map.212
  161.8 1.8 collective-permute-start.34
  164.8 4.8 %collective-permute-done.34 = bf16[56,768]{1,0:T(8,128)(2,1)S(1)} collective-permute-done((bf16[56,768]{1,0:T(8,128)(2,1)}, bf16[56,768]{1,0:T(8,128)(2,1)S(1)}, u32[]{:S(2)}, u32[]{:S(2)}) %collective-permute-start.34) | collective-permute-done | bytes 86048 | tf_op jit(solution)/shard_map/ppermute | solution.py:34
  170.7 2.2 %collective-permute-start.38 = (bf16[96,768]{1,0:T(8,128)(2,1)S(1)}, bf16[96,768]{1,0:T(8,128)(2,1)S(1)}, u32[]{:S(2)}, u32[]{:S(2)}) collective-permute-start(bf16[96,768]{1,0:T(8,128)(2,1)S(1)} %bitcast.55), channel_id=1, source_target_pairs={{0,16},{4,20},{8,24},{12,28},{16,0},{20,4},{24,8},{28,12},{1,17},{... | collective-permute-start | bytes 442376 | tf_op jit(solution)/shard_map/ppermute | solution.py:34
  172.9 4.4 %collective-permute-done.35 = bf16[104,768]{1,0:T(8,128)(2,1)S(1)} collective-permute-done((bf16[104,768]{1,0:T(8,128)(2,1)S(1)}, bf16[104,768]{1,0:T(8,128)(2,1)S(1)}, u32[]{:S(2)}, u32[]{:S(2)}) %collective-permute-start.35) | collective-permute-done | bytes 159776 | tf_op jit(solution)/shard_map/ppermute | solution.py:34
  177.5 1.3 collective-permute-start.36
  180.6 6.7 %collective-permute-done.36.r_2_ = bf16[200,768]{1,0:T(8,128)(2,1)S(1)} collective-permute-done((bf16[200,768]{1,0:T(8,128)(2,1)S(1)}, bf16[200,768]{1,0:T(8,128)(2,1)S(1)}, u32[]{:S(2)}, u32[]{:S(2)}) %collective-permute-start.36) | collective-permute-done | bytes 307232 | tf_op jit(solution)/shard_map/ppermute | solution.py:34
  189.3 1.4 collective-permute-done.39.r_4_
  191.4 2.8 %shard_map.213 = (f32[192,2304]{1,0:T(8,128)}, f32[192,768]{1,0:T(8,128)}) custom-call(s32[2]{0:T(128)} %pad_add_fusion.r_0_, bf16[200,768]{1,0:T(8,128)(2,1)} %copy-done.2, bf16[200,768]{1,0:T(8,128)(2,1)} %copy-done.17, bf16[192,768]{1,0:T(8,128)(2,1)} %bitcast.49, bf16[192,768]{1,0:T(8,128)(2,1)} %copy-done.23), custom_call_target="tpu_custom_call" | custom-call | tf_op jit(solution)/shard_map/pallas_call | solution.py:54
  (187 shorter events, 27.9 us)
Async XLA Ops:
  0.6 15.4 %collective-permute-start.4 = (bf16[128,768]{1,0:T(8,128)(2,1)}, bf16[128,768]{1,0:T(8,128)(2,1)S(1)}, u32[]{:S(2)}, u32[]{:S(2)}) collective-permute-start(bf16[128,768]{1,0:T(8,128)(2,1)} %r_1_.5), channel_id=1, source_target_pairs={{0,2},{1,3},{2,0},{3,1},{4,6},{5,7},{6,4},{7,5},{8,10},{9,11},{10,... | collective-permute-start | bytes 589832 | tf_op jit(solution)/shard_map/ppermute | solution.py:34
  8.4 19.3 %copy-start.4 = (bf16[32,768]{1,0:T(8,128)(2,1)}, bf16[32,768]{1,0:T(8,128)(2,1)S(1)}, u32[]{:S(2)}) copy-start(bf16[32,768]{1,0:T(8,128)(2,1)S(1)} %dynamic_update_slice.11.r_9_.r_8_.r_0_) | copy-start | bytes 147460
  8.4 5.6 %collective-permute-start.1 = (bf16[32,768]{1,0:T(8,128)(2,1)S(1)}, bf16[32,768]{1,0:T(8,128)(2,1)S(1)}, u32[]{:S(2)}, u32[]{:S(2)}) collective-permute-start(bf16[32,768]{1,0:T(8,128)(2,1)S(1)} %dynamic_update_slice.11.r_9_.r_8_.r_0_), channel_id=1, source_target_pairs={{0,2},{1,3},{2,0},{3,1},{4,6},{5,7},{6,4},{7,5},{8,10},{9,11},{10,... | collective-permute-start | bytes 147464 | tf_op jit(solution)/shard_map/ppermute | solution.py:34
  8.7 5.3 %collective-permute-start = (bf16[32,768]{1,0:T(8,128)(2,1)S(1)}, bf16[32,768]{1,0:T(8,128)(2,1)S(1)}, u32[]{:S(2)}, u32[]{:S(2)}) collective-permute-start(bf16[32,768]{1,0:T(8,128)(2,1)S(1)} %dynamic_update_slice.11.r_9_.r_8_.r_0_), channel_id=1, source_target_pairs={{0,1},{1,0},{2,3},{3,2},{4,5},{5,4},{6,7},{7,6},{8,9},{9,8},{10,11... | collective-permute-start | bytes 147464 | tf_op jit(solution)/shard_map/ppermute | solution.py:34
  8.9 8.4 %collective-permute-start.3 = (bf16[128,768]{1,0:T(8,128)(2,1)}, bf16[128,768]{1,0:T(8,128)(2,1)S(1)}, u32[]{:S(2)}, u32[]{:S(2)}) collective-permute-start(bf16[128,768]{1,0:T(8,128)(2,1)} %r_1_.5), channel_id=1, source_target_pairs={{0,1},{1,0},{2,3},{3,2},{4,5},{5,4},{6,7},{7,6},{8,9},{9,8},{10,11... | collective-permute-start | bytes 589832 | tf_op jit(solution)/shard_map/ppermute | solution.py:34
  9.2 9.8 %collective-permute-start.13 = (bf16[192,768]{1,0:T(8,128)(2,1)}, bf16[192,768]{1,0:T(8,128)(2,1)S(1)}, u32[]{:S(2)}, u32[]{:S(2)}) collective-permute-start(bf16[192,768]{1,0:T(8,128)(2,1)} %r_5_.3), channel_id=1, source_target_pairs={{0,2},{1,3},{2,0},{3,1},{4,6},{5,7},{6,4},{7,5},{8,10},{9,11},{10,... | collective-permute-start | bytes 884744 | tf_op jit(solution)/shard_map/ppermute | solution.py:34
  14.0 13.7 %copy-start.11 = (bf16[32,768]{1,0:T(8,128)(2,1)}, bf16[32,768]{1,0:T(8,128)(2,1)S(1)}, u32[]{:S(2)}) copy-start(bf16[32,768]{1,0:T(8,128)(2,1)S(1)} %collective-permute-done.1.r_11_.r_10_.r_2_) | copy-start | bytes 147460
  14.0 4.0 %collective-permute-start.6 = (bf16[288,384]{1,0:T(8,128)(2,1)}, bf16[288,384]{1,0:T(8,128)(2,1)S(1)}, u32[]{:S(2)}, u32[]{:S(2)}) collective-permute-start(bf16[288,384]{1,0:T(8,128)(2,1)} %get-tuple-element.55), channel_id=1, source_target_pairs={{0,1},{1,0},{2,3},{3,2},{4,5},{5,4},{6,7},{7,6},{8,9},{9,8},{10,11... | collective-permute-start | bytes 663560 | tf_op jit(solution)/shard_map/ppermute | solution.py:34
  14.1 1.7 collective-permute-start.2
  15.8 8.5 %collective-permute-start.7 = (bf16[288,384]{1,0:T(8,128)(2,1)}, bf16[288,384]{1,0:T(8,128)(2,1)S(1)}, u32[]{:S(2)}, u32[]{:S(2)}) collective-permute-start(bf16[288,384]{1,0:T(8,128)(2,1)} %get-tuple-element.56), channel_id=1, source_target_pairs={{0,2},{1,3},{2,0},{3,1},{4,6},{5,7},{6,4},{7,5},{8,10},{9,11},{10,... | collective-permute-start | bytes 663560 | tf_op jit(solution)/shard_map/ppermute | solution.py:34
  16.0 11.7 %collective-permute-start.8 = (bf16[288,384]{1,0:T(8,128)(2,1)}, bf16[288,384]{1,0:T(8,128)(2,1)S(1)}, u32[]{:S(2)}, u32[]{:S(2)}) collective-permute-start(bf16[288,384]{1,0:T(8,128)(2,1)} %get-tuple-element.57), channel_id=1, source_target_pairs={{0,3},{1,2},{2,1},{3,0},{4,7},{5,6},{6,5},{7,4},{8,11},{9,10},{10,... | collective-permute-start | bytes 663560 | tf_op jit(solution)/shard_map/ppermute | solution.py:34
  17.3 10.4 %collective-permute-start.5 = (bf16[128,768]{1,0:T(8,128)(2,1)S(1)}, bf16[128,768]{1,0:T(8,128)(2,1)S(1)}, u32[]{:S(2)}, u32[]{:S(2)}) collective-permute-start(bf16[128,768]{1,0:T(8,128)(2,1)S(1)} %collective-permute-done.4.r_3_), channel_id=1, source_target_pairs={{0,1},{1,0},{2,3},{3,2},{4,5},{5,4},{6,7},{7,6},{8,9},{9,8},{10,11... | collective-permute-start | bytes 589832 | tf_op jit(solution)/shard_map/ppermute | solution.py:34
  17.9 23.3 %collective-permute-start.12 = (bf16[192,768]{1,0:T(8,128)(2,1)}, bf16[192,768]{1,0:T(8,128)(2,1)S(1)}, u32[]{:S(2)}, u32[]{:S(2)}) collective-permute-start(bf16[192,768]{1,0:T(8,128)(2,1)} %r_5_.3), channel_id=1, source_target_pairs={{0,1},{1,0},{2,3},{3,2},{4,5},{5,4},{6,7},{7,6},{8,9},{9,8},{10,11... | collective-permute-start | bytes 884744 | tf_op jit(solution)/shard_map/ppermute | solution.py:34
  19.0 25.3 %copy-start.20 = (bf16[192,768]{1,0:T(8,128)(2,1)}, bf16[192,768]{1,0:T(8,128)(2,1)S(1)}, u32[]{:S(2)}) copy-start(bf16[192,768]{1,0:T(8,128)(2,1)S(1)} %collective-permute-done.13.r_6_) | copy-start | bytes 884740
  19.0 25.3 %collective-permute-start.14 = (bf16[192,768]{1,0:T(8,128)(2,1)S(1)}, bf16[192,768]{1,0:T(8,128)(2,1)S(1)}, u32[]{:S(2)}, u32[]{:S(2)}) collective-permute-start(bf16[192,768]{1,0:T(8,128)(2,1)S(1)} %collective-permute-done.13.r_6_), channel_id=1, source_target_pairs={{0,1},{1,0},{2,3},{3,2},{4,5},{5,4},{6,7},{7,6},{8,9},{9,8},{10,11... | collective-permute-start | bytes 884744 | tf_op jit(solution)/shard_map/ppermute | solution.py:34
  37.8 3.4 %collective-permute-start.9 = (bf16[128,192]{1,0:T(8,128)(2,1)}, bf16[128,192]{1,0:T(8,128)(2,1)S(1)}, u32[]{:S(2)}, u32[]{:S(2)}) collective-permute-start(bf16[128,192]{1,0:T(8,128)(2,1)} %get-tuple-element.59), channel_id=1, source_target_pairs={{0,1},{1,0},{2,3},{3,2},{4,5},{5,4},{6,7},{7,6},{8,9},{9,8},{10,11... | collective-permute-start | bytes 147464 | tf_op jit(solution)/shard_map/ppermute | solution.py:34
  38.4 4.5 %collective-permute-start.10 = (bf16[128,192]{1,0:T(8,128)(2,1)}, bf16[128,192]{1,0:T(8,128)(2,1)S(1)}, u32[]{:S(2)}, u32[]{:S(2)}) collective-permute-start(bf16[128,192]{1,0:T(8,128)(2,1)} %get-tuple-element.60), channel_id=1, source_target_pairs={{0,2},{1,3},{2,0},{3,1},{4,6},{5,7},{6,4},{7,5},{8,10},{9,11},{10,... | collective-permute-start | bytes 147464 | tf_op jit(solution)/shard_map/ppermute | solution.py:34
  39.7 4.6 %collective-permute-start.11 = (bf16[128,192]{1,0:T(8,128)(2,1)}, bf16[128,192]{1,0:T(8,128)(2,1)S(1)}, u32[]{:S(2)}, u32[]{:S(2)}) collective-permute-start(bf16[128,192]{1,0:T(8,128)(2,1)} %get-tuple-element.61), channel_id=1, source_target_pairs={{0,3},{1,2},{2,1},{3,0},{4,7},{5,6},{6,5},{7,4},{8,11},{9,10},{10,... | collective-permute-start | bytes 147464 | tf_op jit(solution)/shard_map/ppermute | solution.py:34
  62.5 5.7 %collective-permute-start.16 = (bf16[64,1536]{1,0:T(8,128)(2,1)S(1)}, bf16[64,1536]{1,0:T(8,128)(2,1)S(1)}, u32[]{:S(2)}, u32[]{:S(2)}) collective-permute-start(bf16[64,1536]{1,0:T(8,128)(2,1)S(1)} %bitcast.43), channel_id=1, source_target_pairs={{0,2},{1,3},{2,0},{3,1},{4,6},{5,7},{6,4},{7,5},{8,10},{9,11},{10,... | collective-permute-start | bytes 589832 | tf_op jit(solution)/shard_map/ppermute | solution.py:34
  63.6 4.6 %collective-permute-start.15 = (bf16[64,1536]{1,0:T(8,128)(2,1)S(1)}, bf16[64,1536]{1,0:T(8,128)(2,1)S(1)}, u32[]{:S(2)}, u32[]{:S(2)}) collective-permute-start(bf16[64,1536]{1,0:T(8,128)(2,1)S(1)} %bitcast.44), channel_id=1, source_target_pairs={{0,1},{1,0},{2,3},{3,2},{4,5},{5,4},{6,7},{7,6},{8,9},{9,8},{10,11... | collective-permute-start | bytes 589832 | tf_op jit(solution)/shard_map/ppermute | solution.py:34
  68.2 1.4 collective-permute-start.17
  77.1 2.0 %collective-permute-start.18 = (bf16[128,1536]{1,0:T(8,128)(2,1)}, bf16[128,1536]{1,0:T(8,128)(2,1)S(1)}, u32[]{:S(2)}, u32[]{:S(2)}) collective-permute-start(bf16[128,1536]{1,0:T(8,128)(2,1)} %get-tuple-element.64), channel_id=1, source_target_pairs={{0,1},{1,0},{2,3},{3,2},{4,5},{5,4},{6,7},{7,6},{8,9},{9,8},{10,11... | collective-permute-start | bytes 1179656 | tf_op jit(solution)/shard_map/ppermute | solution.py:34
  80.3 7.0 %collective-permute-start.19 = (bf16[64,1536]{1,0:T(8,128)(2,1)S(1)}, bf16[64,1536]{1,0:T(8,128)(2,1)S(1)}, u32[]{:S(2)}, u32[]{:S(2)}) collective-permute-start(bf16[64,1536]{1,0:T(8,128)(2,1)S(1)} %fusion.9), channel_id=1, source_target_pairs={{0,2},{1,3},{2,0},{3,1},{4,6},{5,7},{6,4},{7,5},{8,10},{9,11},{10,... | collective-permute-start | bytes 589832 | tf_op jit(solution)/shard_map/ppermute | solution.py:34
  103.5 5.9 %collective-permute-start.21 = (bf16[128,768]{1,0:T(8,128)(2,1)}, bf16[128,768]{1,0:T(8,128)(2,1)S(1)}, u32[]{:S(2)}, u32[]{:S(2)}) collective-permute-start(bf16[128,768]{1,0:T(8,128)(2,1)} %get-tuple-element.71.r_1_), channel_id=1, source_target_pairs={{0,2},{1,3},{2,0},{3,1},{4,6},{5,7},{6,4},{7,5},{8,10},{9,11},{10,... | collective-permute-start | bytes 589832 | tf_op jit(solution)/shard_map/ppermute | solution.py:34
  104.5 4.9 %collective-permute-start.20 = (bf16[128,768]{1,0:T(8,128)(2,1)}, bf16[128,768]{1,0:T(8,128)(2,1)S(1)}, u32[]{:S(2)}, u32[]{:S(2)}) collective-permute-start(bf16[128,768]{1,0:T(8,128)(2,1)} %get-tuple-element.71.r_1_), channel_id=1, source_target_pairs={{0,1},{1,0},{2,3},{3,2},{4,5},{5,4},{6,7},{7,6},{8,9},{9,8},{10,11... | collective-permute-start | bytes 589832 | tf_op jit(solution)/shard_map/ppermute | solution.py:34
  109.4 1.4 collective-permute-start.22
  123.5 15.4 %copy-start.19 = (bf16[4,96,384]{2,1,0:T(8,128)(2,1)S(1)}, bf16[4,96,384]{2,1,0:T(8,128)(2,1)}, u32[]{:S(2)}) copy-start(bf16[4,96,384]{2,1,0:T(8,128)(2,1)} %get-tuple-element.86) | copy-start | bytes 884740
  123.5 15.7 %copy-start.18 = (bf16[4,48,768]{2,1,0:T(8,128)(2,1)S(1)}, bf16[4,48,768]{2,1,0:T(8,128)(2,1)}, u32[]{:S(2)}) copy-start(bf16[4,48,768]{2,1,0:T(8,128)(2,1)} %get-tuple-element.88) | copy-start | bytes 884740
  123.5 15.3 %collective-permute-start.25 = (bf16[4,96,384]{2,1,0:T(8,128)(2,1)}, bf16[4,96,384]{2,1,0:T(8,128)(2,1)S(1)}, u32[]{:S(2)}, u32[]{:S(2)}) collective-permute-start(bf16[4,96,384]{2,1,0:T(8,128)(2,1)} %get-tuple-element.87), channel_id=1, source_target_pairs={{0,4},{4,0},{8,12},{12,8},{16,20},{20,16},{24,28},{28,24},{1,5},{5... | collective-permute-start | bytes 884744 | tf_op jit(solution)/shard_map/ppermute | solution.py:34
  124.6 14.7 %collective-permute-start.28 = (bf16[4,48,768]{2,1,0:T(8,128)(2,1)S(1)}, bf16[4,48,768]{2,1,0:T(8,128)(2,1)S(1)}, u32[]{:S(2)}, u32[]{:S(2)}) collective-permute-start(bf16[4,48,768]{2,1,0:T(8,128)(2,1)S(1)} %copy-done.38), channel_id=1, source_target_pairs={{0,4},{4,0},{8,12},{12,8},{16,20},{20,16},{24,28},{28,24},{1,5},{5... | collective-permute-start | bytes 884744 | tf_op jit(solution)/shard_map/ppermute | solution.py:34
  138.8 10.4 %collective-permute-start.23 = (bf16[288,768]{1,0:T(8,128)(2,1)}, bf16[288,768]{1,0:T(8,128)(2,1)S(1)}, u32[]{:S(2)}, u32[]{:S(2)}) collective-permute-start(bf16[288,768]{1,0:T(8,128)(2,1)} %get-tuple-element.83), channel_id=1, source_target_pairs={{0,1},{1,0},{2,3},{3,2},{4,5},{5,4},{6,7},{7,6},{8,9},{9,8},{10,11... | collective-permute-start | bytes 1327112 | tf_op jit(solution)/shard_map/ppermute | solution.py:34
  139.0 6.8 %collective-permute-start.26 = (bf16[2,96,384]{2,1,0:T(8,128)(2,1)S(1)}, bf16[2,96,384]{2,1,0:T(8,128)(2,1)S(1)}, u32[]{:S(2)}, u32[]{:S(2)}) collective-permute-start(bf16[2,96,384]{2,1,0:T(8,128)(2,1)S(1)} %slice.158), channel_id=1, source_target_pairs={{0,8},{4,12},{8,0},{12,4},{16,24},{20,28},{24,16},{28,20},{1,9},{5... | collective-permute-start | bytes 442376 | tf_op jit(solution)/shard_map/ppermute | solution.py:34
  139.3 9.1 %collective-permute-start.29 = (bf16[2,48,768]{2,1,0:T(8,128)(2,1)S(1)}, bf16[2,48,768]{2,1,0:T(8,128)(2,1)S(1)}, u32[]{:S(2)}, u32[]{:S(2)}) collective-permute-start(bf16[2,48,768]{2,1,0:T(8,128)(2,1)S(1)} %slice.164), channel_id=1, source_target_pairs={{0,8},{4,12},{8,0},{12,4},{16,24},{20,28},{24,16},{28,20},{1,9},{5... | collective-permute-start | bytes 442376 | tf_op jit(solution)/shard_map/ppermute | solution.py:34
  145.8 17.9 %copy-start = (bf16[128,768]{1,0:T(8,128)(2,1)S(1)}, bf16[128,768]{1,0:T(8,128)(2,1)}, u32[]{:S(2)}) copy-start(bf16[128,768]{1,0:T(8,128)(2,1)} %r_1_.5) | copy-start | bytes 589828
  145.8 17.9 %copy-start.15 = (f32[128,768]{1,0:T(8,128)S(1)}, f32[128,768]{1,0:T(8,128)}, u32[]{:S(2)}) copy-start(f32[128,768]{1,0:T(8,128)} %get-tuple-element.82) | copy-start | bytes 1179652
  145.9 5.8 %collective-permute-start.27 = (bf16[1,96,384]{2,1,0:T(8,128)(2,1)S(1)}, bf16[1,96,384]{2,1,0:T(8,128)(2,1)S(1)}, u32[]{:S(2)}, u32[]{:S(2)}) collective-permute-start(bf16[1,96,384]{2,1,0:T(8,128)(2,1)S(1)} %slice.203), channel_id=1, source_target_pairs={{0,16},{4,20},{8,24},{12,28},{16,0},{20,4},{24,8},{28,12},{1,17},{... | collective-permute-start | bytes 221192 | tf_op jit(solution)/shard_map/ppermute | solution.py:34
  148.5 6.3 %collective-permute-start.30 = (bf16[1,48,768]{2,1,0:T(8,128)(2,1)S(1)}, bf16[1,48,768]{2,1,0:T(8,128)(2,1)S(1)}, u32[]{:S(2)}, u32[]{:S(2)}) collective-permute-start(bf16[1,48,768]{2,1,0:T(8,128)(2,1)S(1)} %slice.206), channel_id=1, source_target_pairs={{0,16},{4,20},{8,24},{12,28},{16,0},{20,4},{24,8},{28,12},{1,17},{... | collective-permute-start | bytes 221192 | tf_op jit(solution)/shard_map/ppermute | solution.py:34
  149.4 8.7 %collective-permute-start.24 = (bf16[160,768]{1,0:T(8,128)(2,1)S(1)}, bf16[160,768]{1,0:T(8,128)(2,1)S(1)}, u32[]{:S(2)}, u32[]{:S(2)}) collective-permute-start(bf16[160,768]{1,0:T(8,128)(2,1)S(1)} %pad_maximum_fusion.3), channel_id=1, source_target_pairs={{0,2},{1,3},{2,0},{3,1},{4,6},{5,7},{6,4},{7,5},{8,10},{9,11},{10,... | collective-permute-start | bytes 737288 | tf_op jit(solution)/shard_map/ppermute | solution.py:34
  154.9 4.0 %collective-permute-start.31 = (bf16[24,576]{1,0:T(8,128)(2,1)S(1)}, bf16[24,576]{1,0:T(8,128)(2,1)S(1)}, u32[]{:S(2)}, u32[]{:S(2)}) collective-permute-start(bf16[24,576]{1,0:T(8,128)(2,1)S(1)} %pad_maximum_fusion.8), channel_id=1, source_target_pairs={{0,1},{1,0},{2,3},{3,2},{4,5},{5,4},{6,7},{7,6},{8,9},{9,8},{10,11... | collective-permute-start | bytes 82952 | tf_op jit(solution)/shard_map/ppermute | solution.py:34
  155.0 4.0 %collective-permute-start.32 = (bf16[24,576]{1,0:T(8,128)(2,1)S(1)}, bf16[24,576]{1,0:T(8,128)(2,1)S(1)}, u32[]{:S(2)}, u32[]{:S(2)}) collective-permute-start(bf16[24,576]{1,0:T(8,128)(2,1)S(1)} %pad_maximum_fusion.9), channel_id=1, source_target_pairs={{0,2},{1,3},{2,0},{3,1},{4,6},{5,7},{6,4},{7,5},{8,10},{9,11},{10,... | collective-permute-start | bytes 82952 | tf_op jit(solution)/shard_map/ppermute | solution.py:34
  156.1 3.3 %collective-permute-start.33 = (bf16[24,576]{1,0:T(8,128)(2,1)S(1)}, bf16[24,576]{1,0:T(8,128)(2,1)S(1)}, u32[]{:S(2)}, u32[]{:S(2)}) collective-permute-start(bf16[24,576]{1,0:T(8,128)(2,1)S(1)} %pad_maximum_fusion.10), channel_id=1, source_target_pairs={{0,3},{1,2},{2,1},{3,0},{4,7},{5,6},{6,5},{7,4},{8,11},{9,10},{10,... | collective-permute-start | bytes 82952 | tf_op jit(solution)/shard_map/ppermute | solution.py:34
  161.8 16.9 %copy-start.14 = (f32[128,768]{1,0:T(8,128)S(1)}, f32[128,768]{1,0:T(8,128)}, u32[]{:S(2)}) copy-start(f32[128,768]{1,0:T(8,128)} %get-tuple-element.70) | copy-start | bytes 1179652
  161.8 8.9 %collective-permute-start.37 = (bf16[48,768]{1,0:T(8,128)(2,1)}, bf16[48,768]{1,0:T(8,128)(2,1)S(1)}, u32[]{:S(2)}, u32[]{:S(2)}) collective-permute-start(bf16[48,768]{1,0:T(8,128)(2,1)} %get-tuple-element.91), channel_id=1, source_target_pairs={{0,8},{4,12},{8,0},{12,4},{16,24},{20,28},{24,16},{28,20},{1,9},{5... | collective-permute-start | bytes 221192 | tf_op jit(solution)/shard_map/ppermute | solution.py:34
  161.8 7.8 %collective-permute-start.34 = (bf16[56,768]{1,0:T(8,128)(2,1)}, bf16[56,768]{1,0:T(8,128)(2,1)S(1)}, u32[]{:S(2)}, u32[]{:S(2)}) collective-permute-start(bf16[56,768]{1,0:T(8,128)(2,1)} %get-tuple-element.90), channel_id=1, source_target_pairs={{0,16},{4,20},{8,24},{12,28},{16,0},{20,4},{24,8},{28,12},{1,17},{... | collective-permute-start | bytes 258056 | tf_op jit(solution)/shard_map/ppermute | solution.py:34
  170.4 6.9 %collective-permute-start.35 = (bf16[104,768]{1,0:T(8,128)(2,1)S(1)}, bf16[104,768]{1,0:T(8,128)(2,1)S(1)}, u32[]{:S(2)}, u32[]{:S(2)}) collective-permute-start(bf16[104,768]{1,0:T(8,128)(2,1)S(1)} %pad_maximum_fusion.4), channel_id=1, source_target_pairs={{0,8},{4,12},{8,0},{12,4},{16,24},{20,28},{24,16},{28,20},{1,9},{5... | collective-permute-start | bytes 479240 | tf_op jit(solution)/shard_map/ppermute | solution.py:34
  170.7 9.0 %collective-permute-start.38 = (bf16[96,768]{1,0:T(8,128)(2,1)S(1)}, bf16[96,768]{1,0:T(8,128)(2,1)S(1)}, u32[]{:S(2)}, u32[]{:S(2)}) collective-permute-start(bf16[96,768]{1,0:T(8,128)(2,1)S(1)} %bitcast.55), channel_id=1, source_target_pairs={{0,16},{4,20},{8,24},{12,28},{16,0},{20,4},{24,8},{28,12},{1,17},{... | collective-permute-start | bytes 442376 | tf_op jit(solution)/shard_map/ppermute | solution.py:34
  177.5 9.8 %collective-permute-start.36 = (bf16[200,768]{1,0:T(8,128)(2,1)S(1)}, bf16[200,768]{1,0:T(8,128)(2,1)S(1)}, u32[]{:S(2)}, u32[]{:S(2)}) collective-permute-start(bf16[200,768]{1,0:T(8,128)(2,1)S(1)} %pad_maximum_fusion.r_1_), channel_id=1, source_target_pairs={{0,4},{4,0},{8,12},{12,8},{16,20},{20,16},{24,28},{28,24},{1,5},{5... | collective-permute-start | bytes 921608 | tf_op jit(solution)/shard_map/ppermute | solution.py:34
  179.7 11.0 %collective-permute-start.39 = (bf16[192,768]{1,0:T(8,128)(2,1)S(1)}, bf16[192,768]{1,0:T(8,128)(2,1)S(1)}, u32[]{:S(2)}, u32[]{:S(2)}) collective-permute-start(bf16[192,768]{1,0:T(8,128)(2,1)S(1)} %bitcast.48), channel_id=1, source_target_pairs={{0,4},{4,0},{8,12},{12,8},{16,20},{20,16},{24,28},{28,24},{1,5},{5... | collective-permute-start | bytes 884744 | tf_op jit(solution)/shard_map/ppermute | solution.py:34
  (31 other events, 154.0 us)
